TPU v7x, 256 devices: a whole 4x4x8 slice. The times are simulated.
256 devices in a mesh: energy: 16 (over z, core), cell: 16 (over y, x).
Axes of the slice: x: 4, y: 4, z: 8, core: 2. Of those that a mesh axis runs over, the one named last changes fastest.
Arguments:
- green: bfloat16 [4, 96, 32, 16, 512], P(None, 'energy', 'cell'), may hold values from -6 to 6
- screened: bfloat16 [4, 96, 32, 16, 512], P(None, 'energy', None, 'cell'), may hold values from -6 to 6
- cell_map: int32 [32], replicated, may hold values from 0 to 31, each once
- shift_table: int32 [16, 16, 3], replicated, may hold values from 0 to 5, as said below
- shift_count: int32 [16, 16], replicated, may hold values from 1 to 3, as said below
Outputs:
- sigma: float32 [4, 96, 32, 16, 512], P(None, 'energy', 'cell')
Inputs may be any that keep to these rules, and one draw needn't show every extreme that they name: `shift_table`: offsets of requested energies within the source group; slots c >= shift_count[g, s] are not read. `shift_count`: some destination group requests 3 energies from every source group. `cell_map`: each cell stands at exactly one position.
All inputs are finite; a program needn't handle non-finite values.
Results may differ from a plain program's by a relative error of at most 0.0003.
Values may be sent and summed in bfloat16 or wider, within the bound.
A program may use at most 128 MiB of HBM per device.

v0:
```python
import jax
import jax.numpy as jnp
from jax import lax
from jax.sharding import PartitionSpec as P

SCALE = 0.2


def per_device(green, screened, cell_map, shift_table, shift_count):
    groups = lax.axis_size("energy")
    cell_count = lax.axis_size("cell")
    per_energy = green.shape[1]
    per_cell = green.shape[2]
    width = green.shape[4]
    slot_count = shift_table.shape[2]
    wanted = jnp.transpose(cell_map.reshape(cell_count, per_cell)).reshape(-1)
    outgoing = jnp.take(screened, wanted, axis=2)
    outgoing = outgoing.reshape(4, per_energy, per_cell, cell_count, screened.shape[3], width)
    arrived = lax.all_to_all(outgoing, "cell", split_axis=3, concat_axis=3, tiled=True)
    owned = arrived.reshape(4, per_energy, per_cell, green.shape[3], width)
    whole = lax.all_gather(green, "energy", axis=1, tiled=True)
    padding = jnp.zeros((4, per_energy) + whole.shape[2:], whole.dtype)
    padded = jnp.concatenate([padding, whole], axis=1)
    group = lax.axis_index("energy")
    first = group * per_energy
    table_row = shift_table[group]
    counts = shift_count[group]
    every = lax.all_gather(owned, "energy", axis=1, tiled=True)

    def values_of(energy):
        return lax.dynamic_index_in_dim(every, energy, 1, keepdims=False)

    def turn(totals, source):
        sums = list(totals)
        for slot in range(slot_count):
            energy = source * per_energy + table_row[source, slot]
            live = (slot < counts[source]).astype(jnp.float32)
            start = jnp.maximum(first - energy, -per_energy) + per_energy
            window = lax.dynamic_slice_in_dim(padded, start, per_energy, 1)
            value = values_of(energy)
            for kind in range(2):
                g_real = window[2 * kind].astype(jnp.float32)
                g_imag = window[2 * kind + 1].astype(jnp.float32)
                w_real = value[2 * kind].astype(jnp.float32)[None] * live
                w_imag = value[2 * kind + 1].astype(jnp.float32)[None] * live
                sums[2 * kind] = sums[2 * kind] - (g_real * w_imag + g_imag * w_real)
                sums[2 * kind + 1] = sums[2 * kind + 1] + (g_real * w_real - g_imag * w_imag)
        return (tuple(sums), None)

    zeros = jnp.zeros(green.shape[1:], jnp.float32)
    totals, _ = lax.scan(turn, (zeros, zeros, zeros, zeros), jnp.arange(groups, dtype=jnp.int32))
    return jnp.stack(totals, axis=0) * SCALE


def solution(mesh):
    placed = (
        P(None, "energy", "cell", None, None),
        P(None, "energy", None, "cell", None),
        P(),
        P(),
        P(),
    )
    return jax.shard_map(
        per_device,
        mesh=mesh,
        in_specs=placed,
        out_specs=P(None, "energy", "cell", None, None),
        check_vma=False,
    )
```

profile of v0, /device:TPU:1, one launch (start us, length us, event | category | flops | bytes accessed | tf_op | source)
XLA Modules:
  0.0 408.7 jit_solution(6469236370796020394)
XLA Ops:
  12.3 21.0 %all_to_all.5 = bf16[4,6,2,16,1,512]{5,2,1,0,4,3:T(2,128)(2,1)} all-to-all(bf16[4,6,2,16,1,512]{5,2,1,0,4,3:T(2,128)(2,1)S(1)} %broadcast_select_fusion), channel_id=1, replica_groups=mesh['energy'=16,'cell'=16] {'cell'}, dimensions={3} | all-to-all | bytes 1572864 | tf_op jit(solution)/shard_map/all_to_all | solution.py:19
  34.1 55.1 %all-gather.4.cloned.1.call-done = bf16[4,96,2,16,512]{4,3,2,1,0:T(8,128)(2,1)} async-done(((bf16[4,6,2,16,512]{4,3,2,1,0:T(8,128)(2,1)}), bf16[4,96,2,16,512]{4,3,2,1,0:T(8,128)(2,1)}) %all-gather.4.cloned.1.call-update) | async-done | bytes 12582928 | tf_op jit(solution)/shard_map/all_gather | solution.py:21
  89.1 11.3 %concatenate.3 = bf16[4,102,2,16,512]{4,3,2,1,0:T(8,128)(2,1)} pad(bf16[4,96,2,16,512]{4,3,2,1,0:T(8,128)(2,1)} %all-gather.4.cloned.1.call-done, bf16[]{:T(256)} %constant.96.clone.1), padding=0_0x6_0x0_0x0_0x0_0 | pad | bytes 25952258 | tf_op jit(solution)/shard_map/concatenate | solution.py:23
  100.5 64.7 %all-gather.6.cloned.1.call-done = bf16[4,96,2,16,1,512]{5,2,1,0,4,3:T(2,128)(2,1)} async-done(((bf16[4,6,2,16,1,512]{5,2,1,0,4,3:T(2,128)(2,1)}), bf16[4,96,2,16,1,512]{5,2,1,0,4,3:T(2,128)(2,1)}) %all-gather.6.cloned.1.call-update) | async-done | bytes 12582928 | tf_op jit(solution)/shard_map/all_gather | solution.py:28
  165.2 23.7 %copy.15 = bf16[4,96,2,16,512]{4,3,2,1,0:T(8,128)(2,1)} copy(bf16[4,96,2,16,512]{4,2,1,0,3:T(2,128)(2,1)} %bitcast.179) | data formatting | bytes 25165824
  188.9 211.6 %while.20 = (s32[]{:T(128)}, f32[6,2,16,512]{3,2,1,0:T(8,128)S(1)}, f32[6,2,16,512]{3,2,1,0:T(8,128)S(1)}, f32[6,2,16,512]{3,2,1,0:T(8,128)S(1)}, f32[6,2,16,512...) while((s32[]{:T(128)}, f32[6,2,16,512]{3,2,1,0:T(8,128)S(1)}, ...), condition=%wide.region_1.2_spmd.clone, body=%wide.region_0.1_spmd.clone.sunk | while | flops 6684718 | bytes 7471924 | solution.py:51
  198.6 1.8 fusion.28
  200.4 1.8 fusion.27
  211.8 1.8 fusion.28
  213.6 1.8 fusion.27
  225.1 1.8 fusion.28
  226.9 1.8 fusion.27
  238.3 1.8 fusion.28
  251.5 1.8 fusion.28
  253.3 1.8 fusion.27
  264.7 1.8 fusion.28
  266.5 1.8 fusion.27
  277.9 1.8 fusion.28
  291.2 1.8 fusion.28
  293.0 1.8 fusion.27
  304.4 1.8 fusion.28
  317.6 1.8 fusion.28
  319.4 1.8 fusion.27
  330.9 1.8 fusion.28
  332.7 1.8 fusion.27
  344.1 1.8 fusion.28
  357.3 1.8 fusion.28
  359.1 1.8 fusion.27
  370.5 1.8 fusion.28
  372.3 1.8 fusion.27
  383.7 1.8 fusion.28
  397.0 1.8 fusion.28
  (94 shorter events, 66.8 us)
Async XLA Ops:
  6.5 26.8 %copy-start = (s32[16,16,3]{1,0,2:T(8,128)S(1)}, s32[16,16,3]{1,0,2:T(8,128)}, u32[]{:S(2)}) copy-start(s32[16,16,3]{1,0,2:T(8,128)} %param.10) | copy-start | bytes 9220
  6.5 82.6 %all-gather.4.cloned.1.call-start = ((), (), s32[]{:S(2)}) async-start(), calls=%async_computation.1 | async-start | bytes 13369344 | tf_op jit(solution)/shard_map/all_gather | solution.py:21
  7.3 157.9 %all-gather.6.cloned.1.call-start = ((), (), s32[]{:S(2)}) async-start(), calls=%async_computation.2 | async-start | bytes 13369344 | tf_op jit(solution)/shard_map/all_gather | solution.py:28
Sparse Core Ops, SparseCore 0:
  9.2 79.8 all-gather.3
  91.0 74.1 all-gather.5
where the time goes:
time: 413 us; the launch traced here: 409 us
  waiting for transfers between devices  121 us (29%)
  loops' own time  106 us (26%)
  other arithmetic  76.5 us (19%)
  local copies, waits for them, and re-layouts  71.2 us (17%)
  blocking collectives  21 us (5%)
  between operations  13.5 us (3%)
    another operation x1, loops' own time, per_device(): lax.scan(turn, (zeros, zeros, zeros, zeros), jnp.arange(groups, dtype=jnp...  106 us
    all_gather x1, waiting for transfers between devices, per_device(): every = lax.all_gather(owned, 'energy', axis=1, tiled=True)  64.7 us
    add x32, other arithmetic, turn(): sums[2 * kind + 1] + (g_real * w_real - g_imag * w_imag)  57.2 us
    all_gather x1, waiting for transfers between devices, per_device(): whole = lax.all_gather(green, 'energy', axis=1, tiled=True)  55.1 us
    unnamed x5, local copies, waits for them, and re-layouts  25.5 us
    all_to_all x1, blocking collectives, per_device(): lax.all_to_all(outgoing, 'cell', split_axis=3, concat_axis=3, tiled=True)  21 us
    mul x16, other arithmetic, turn(): w_imag = value[2 * kind + 1].astype(jnp.float32)[None] * live  16.9 us
    concatenate x1, local copies, waits for them, and re-layouts, per_device(): padded = jnp.concatenate([padding, whole], axis=1)  11.3 us
  transfers between devices with their start and end apart: 2, of which 2 were waited for; matrix products, arithmetic and copies ran while one was open for 4% of the time, Pallas kernels for 0%

commit v1 on v0

v1 whole, which is shorter than its diff:
```python
import functools

import jax
import jax.numpy as jnp
from jax import lax
from jax.experimental import pallas as pl
from jax.experimental.pallas import tpu as pltpu
from jax.sharding import PartitionSpec as P

SCALE = 0.2
LANES = 128


def term_lists(shift_table, shift_count, group, per_energy):
    groups, slot_count = shift_table.shape[1], shift_table.shape[2]
    total = groups * slot_count
    base = group * per_energy
    table_row = shift_table[group]
    counts = shift_count[group]
    source = lax.broadcasted_iota(jnp.int32, (groups, slot_count), 0)
    slot = lax.broadcasted_iota(jnp.int32, (groups, slot_count), 1)
    energies = (source * per_energy + table_row).reshape(total)
    live = (slot < counts[:, None]).reshape(total)
    local = lax.broadcasted_iota(jnp.int32, (per_energy, 1), 0)
    valid = live[None, :] & (energies[None, :] <= base + local)
    place = jnp.cumsum(valid.astype(jnp.int32), axis=1) - 1
    target = lax.broadcasted_iota(jnp.int32, (1, 1, total), 2)
    hit = valid[:, :, None] & (place[:, :, None] == target)
    lists = jnp.sum(jnp.where(hit, energies[None, :, None], 0), axis=1)
    sizes = jnp.sum(valid.astype(jnp.int32), axis=1)
    head = jnp.concatenate([sizes, base[None]]).astype(jnp.int32)
    return head, lists.reshape(-1).astype(jnp.int32)


def conv_kernel(per_energy, total, head_ref, lists_ref, g_ref, w_ref, o_ref):
    base = head_ref[per_energy]
    rows, width = g_ref.shape[2], g_ref.shape[3]
    for chunk in range(width // LANES):
        lanes = pl.ds(chunk * LANES, LANES)
        for e in range(per_energy):
            def body(t, acc, e=e, lanes=lanes):
                w = lists_ref[e * total + t]
                u = base + e - w
                out = list(acc)
                for kind in range(2):
                    gr = g_ref[2 * kind, u, :, lanes].astype(jnp.float32)
                    gi = g_ref[2 * kind + 1, u, :, lanes].astype(jnp.float32)
                    wr = w_ref[2 * kind, w, :, lanes].astype(jnp.float32)
                    wi = w_ref[2 * kind + 1, w, :, lanes].astype(jnp.float32)
                    out[2 * kind] = out[2 * kind] - (gr * wi + gi * wr)
                    out[2 * kind + 1] = out[2 * kind + 1] + (gr * wr - gi * wi)
                return tuple(out)

            zero = jnp.zeros((rows, LANES), jnp.float32)
            acc = lax.fori_loop(0, head_ref[e], body, (zero,) * 4)
            for comp in range(4):
                o_ref[comp, e, :, lanes] = acc[comp] * SCALE


def convolve(head, lists, whole, every, per_energy):
    comps, energies, positions, rows, width = whole.shape
    total = lists.shape[0] // per_energy
    in_block = pl.BlockSpec(
        (comps, energies, pl.squeezed, rows, width), lambda p, h, l: (0, 0, p, 0, 0)
    )
    out_block = pl.BlockSpec(
        (comps, per_energy, pl.squeezed, rows, width), lambda p, h, l: (0, 0, p, 0, 0)
    )
    return pl.pallas_call(
        functools.partial(conv_kernel, per_energy, total),
        out_shape=jax.ShapeDtypeStruct((comps, per_energy, positions, rows, width), jnp.float32),
        grid_spec=pltpu.PrefetchScalarGridSpec(
            num_scalar_prefetch=2,
            grid=(positions,),
            in_specs=[in_block, in_block],
            out_specs=out_block,
        ),
        compiler_params=pltpu.CompilerParams(vmem_limit_bytes=48 * 1024 * 1024),
    )(head, lists, whole, every)


def per_device(green, screened, cell_map, shift_table, shift_count):
    cell_count = lax.axis_size("cell")
    per_energy = green.shape[1]
    per_cell = green.shape[2]
    width = green.shape[4]
    wanted = jnp.transpose(cell_map.reshape(cell_count, per_cell)).reshape(-1)
    outgoing = jnp.take(screened, wanted, axis=2)
    outgoing = outgoing.reshape(4, per_energy, per_cell, cell_count, screened.shape[3], width)
    arrived = lax.all_to_all(outgoing, "cell", split_axis=3, concat_axis=3, tiled=True)
    owned = arrived.reshape(4, per_energy, per_cell, green.shape[3], width)
    whole = lax.all_gather(green, "energy", axis=1, tiled=True)
    every = lax.all_gather(owned, "energy", axis=1, tiled=True)
    group = lax.axis_index("energy")
    head, lists = term_lists(shift_table, shift_count, group, per_energy)
    return convolve(head, lists, whole, every, per_energy)


def solution(mesh):
    placed = (
        P(None, "energy", "cell", None, None),
        P(None, "energy", None, "cell", None),
        P(),
        P(),
        P(),
    )
    return jax.shard_map(
        per_device,
        mesh=mesh,
        in_specs=placed,
        out_specs=P(None, "energy", "cell", None, None),
        check_vma=False,
    )
```

time: 413 us -> 202 us (0.49)
  the two profiles are of different devices: /device:TPU:1 before, /device:TPU:193 now
where the time goes in v1:
time: 202 us
  waiting for transfers between devices  125 us (62%)
  Pallas kernels  34.9 us (17%)
  blocking collectives  20.1 us (10%)
  between operations  13.5 us (7%)
  local copies, waits for them, and re-layouts  6.45 us (3%)
    all_gather x1, waiting for transfers between devices, per_device(): every = lax.all_gather(owned, 'energy', axis=1, tiled=True)  76.1 us
    all_gather x1, waiting for transfers between devices, per_device(): whole = lax.all_gather(green, 'energy', axis=1, tiled=True)  48.5 us
    pallas_call x1, Pallas kernels, convolve(): pl.pallas_call(functools.partial(conv_kernel, per_energy, total), out_sha...  34.9 us
    all_to_all x1, blocking collectives, per_device(): lax.all_to_all(outgoing, 'cell', split_axis=3, concat_axis=3, tiled=True)  20.1 us
  transfers between devices with their start and end apart: 2, of which 2 were waited for; matrix products, arithmetic and copies ran while one was open for 4% of the time, Pallas kernels for 0%

profile of v1, /device:TPU:193, one launch (start us, length us, event | category | flops | bytes accessed | tf_op | source)
XLA Modules:
  0.0 202.0 jit_solution(11093654245246030751)
XLA Ops:
  6.5 0.0 copy-start
  6.5 0.0 all-gather.4.cloned.1.call-start
  6.5 0.7 all-gather.4.cloned.1.call-update
  7.3 0.0 all-gather.6.cloned.1.call-start
  7.3 0.7 reshape.183
  8.0 0.1 copy.21
  8.1 0.1 reshape.184
  8.2 1.8 copy.26
  10.0 1.3 gather_fusion
  11.3 1.0 broadcast_select_fusion
  12.3 20.1 %all_to_all.5 = bf16[4,6,2,16,1,512]{5,2,1,0,4,3:T(2,128)(2,1)S(1)} all-to-all(bf16[4,6,2,16,1,512]{5,2,1,0,4,3:T(2,128)(2,1)S(1)} %broadcast_select_fusion), channel_id=1, replica_groups=mesh['energy'=16,'cell'=16] {'cell'}, dimensions={3} | all-to-all | bytes 1572864 | tf_op jit(solution)/shard_map/all_to_all | solution.py:90
  32.3 1.3 copy.23
  33.6 0.0 all-gather.6.cloned.1.call-update
  33.7 0.7 dynamic-slice_bitcast_fusion
  34.4 0.1 iota_compare_fusion.1
  34.4 0.1 lt.47
  34.5 0.0 copy-done
  34.6 0.1 copy.19
  34.6 0.1 squeeze.3
  34.7 0.1 iota.28
  34.8 0.1 iota.29
  34.9 0.1 fusion.2
  35.0 0.2 reduce_window_sum.11
  35.2 0.2 select_reduce_fusion
  35.4 0.1 reshape.182.lists_ref
  35.5 0.1 convert_reduce_fusion
  35.6 0.1 pad_add_fusion.head_ref
  35.7 48.5 %all-gather.4.cloned.1.call-done.g_ref = bf16[4,96,2,16,512]{4,3,2,1,0:T(8,128)(2,1)} async-done(((bf16[4,6,2,16,512]{4,3,2,1,0:T(8,128)(2,1)}), bf16[4,96,2,16,512]{4,3,2,1,0:T(8,128)(2,1)}) %all-gather.4.cloned.1.call-update) | async-done | bytes 12582928 | tf_op jit(solution)/shard_map/all_gather | solution.py:92
  84.2 76.1 %all-gather.6.cloned.1.call-done = bf16[4,96,2,16,1,512]{5,3,2,1,0,4:T(8,128)(2,1)} async-done(((bf16[4,6,2,16,1,512]{5,3,2,1,0,4:T(8,128)(2,1)}), bf16[4,96,2,16,1,512]{5,3,2,1,0,4:T(8,128)(2,1)}) %all-gather.6.cloned.1.call-update) | async-done | bytes 12582928 | tf_op jit(solution)/shard_map/all_gather | solution.py:93
  160.3 34.9 %shard_map.55 = f32[4,6,2,16,512]{4,3,2,1,0:T(8,128)} custom-call(s32[7]{0:T(128)S(1)} %pad_add_fusion.head_ref, s32[288]{0:T(512)S(1)} %reshape.182.lists_ref, bf16[4,96,2,16,512]{4,3,2,1,0:T(8,128)(2,1)} %all-gather.4.cloned.1.call-done.g_ref, bf16[4,96,2,16,512]{4,3,2,1,0:T(8,128)(2,1)} %bitcast.14), custom_call_target="tpu_custom_call" | custom-call | tf_op jit(solution)/shard_map/pallas_call | solution.py:69
  (8 shorter events, 0.1 us)
Async XLA Ops:
  6.5 28.0 %copy-start = (s32[16,16,3]{1,0,2:T(8,128)S(1)}, s32[16,16,3]{1,0,2:T(8,128)}, u32[]{:S(2)}) copy-start(s32[16,16,3]{1,0,2:T(8,128)} %param.8) | copy-start | bytes 9220
  6.5 77.6 %all-gather.4.cloned.1.call-start = ((), (), s32[]{:S(2)}) async-start(), calls=%async_computation.1 | async-start | bytes 13369344 | tf_op jit(solution)/shard_map/all_gather | solution.py:92
  7.3 153.0 %all-gather.6.cloned.1.call-start = ((), (), s32[]{:S(2)}) async-start(), calls=%async_computation.2 | async-start | bytes 13369344 | tf_op jit(solution)/shard_map/all_gather | solution.py:93
Sparse Core Ops, SparseCore 0:
  9.2 74.9 all-gather.3
  86.0 74.1 all-gather.5

commit v2 on v1

--- a/solution.py
+++ b/solution.py
@@ -29,10 +29,12 @@
     lists = jnp.sum(jnp.where(hit, energies[None, :, None], 0), axis=1)
     sizes = jnp.sum(valid.astype(jnp.int32), axis=1)
     head = jnp.concatenate([sizes, base[None]]).astype(jnp.int32)
-    return head, lists.reshape(-1).astype(jnp.int32)
+    slots = jnp.remainder(group - lists // per_energy, groups)
+    places = slots * per_energy + jnp.remainder(lists, per_energy)
+    return head, lists.reshape(-1).astype(jnp.int32), places.reshape(-1).astype(jnp.int32)
 
 
-def conv_kernel(per_energy, total, head_ref, lists_ref, g_ref, w_ref, o_ref):
+def conv_kernel(per_energy, total, head_ref, lists_ref, places_ref, g_ref, w_ref, o_ref):
     base = head_ref[per_energy]
     rows, width = g_ref.shape[2], g_ref.shape[3]
     for chunk in range(width // LANES):
@@ -41,12 +43,13 @@
             def body(t, acc, e=e, lanes=lanes):
                 w = lists_ref[e * total + t]
                 u = base + e - w
+                v = places_ref[e * total + t]
                 out = list(acc)
                 for kind in range(2):
                     gr = g_ref[2 * kind, u, :, lanes].astype(jnp.float32)
                     gi = g_ref[2 * kind + 1, u, :, lanes].astype(jnp.float32)
-                    wr = w_ref[2 * kind, w, :, lanes].astype(jnp.float32)
-                    wi = w_ref[2 * kind + 1, w, :, lanes].astype(jnp.float32)
+                    wr = w_ref[2 * kind, v, :, lanes].astype(jnp.float32)
+                    wi = w_ref[2 * kind + 1, v, :, lanes].astype(jnp.float32)
                     out[2 * kind] = out[2 * kind] - (gr * wi + gi * wr)
                     out[2 * kind + 1] = out[2 * kind + 1] + (gr * wr - gi * wi)
                 return tuple(out)
@@ -57,26 +60,26 @@
                 o_ref[comp, e, :, lanes] = acc[comp] * SCALE
 
 
-def convolve(head, lists, whole, every, per_energy):
+def convolve(head, lists, places, whole, every, per_energy):
     comps, energies, positions, rows, width = whole.shape
     total = lists.shape[0] // per_energy
     in_block = pl.BlockSpec(
-        (comps, energies, pl.squeezed, rows, width), lambda p, h, l: (0, 0, p, 0, 0)
+        (comps, energies, pl.squeezed, rows, width), lambda p, *_: (0, 0, p, 0, 0)
     )
     out_block = pl.BlockSpec(
-        (comps, per_energy, pl.squeezed, rows, width), lambda p, h, l: (0, 0, p, 0, 0)
+        (comps, per_energy, pl.squeezed, rows, width), lambda p, *_: (0, 0, p, 0, 0)
     )
     return pl.pallas_call(
         functools.partial(conv_kernel, per_energy, total),
         out_shape=jax.ShapeDtypeStruct((comps, per_energy, positions, rows, width), jnp.float32),
         grid_spec=pltpu.PrefetchScalarGridSpec(
-            num_scalar_prefetch=2,
+            num_scalar_prefetch=3,
             grid=(positions,),
             in_specs=[in_block, in_block],
             out_specs=out_block,
         ),
         compiler_params=pltpu.CompilerParams(vmem_limit_bytes=48 * 1024 * 1024),
-    )(head, lists, whole, every)
+    )(head, lists, places, whole, every)
 
 
 def per_device(green, screened, cell_map, shift_table, shift_count):
@@ -90,10 +93,25 @@
     arrived = lax.all_to_all(outgoing, "cell", split_axis=3, concat_axis=3, tiled=True)
     owned = arrived.reshape(4, per_energy, per_cell, green.shape[3], width)
     whole = lax.all_gather(green, "energy", axis=1, tiled=True)
-    every = lax.all_gather(owned, "energy", axis=1, tiled=True)
+    every = ring_gather(owned, "energy")
     group = lax.axis_index("energy")
-    head, lists = term_lists(shift_table, shift_count, group, per_energy)
-    return convolve(head, lists, whole, every, per_energy)
+    head, lists, places = term_lists(shift_table, shift_count, group, per_energy)
+    return convolve(head, lists, places, whole, every, per_energy)
+
+
+def ring_gather(block, axis):
+    n = lax.axis_size(axis)
+    forward = [(i, (i + 1) % n) for i in range(n)]
+    backward = [(i, (i - 1) % n) for i in range(n)]
+    ahead, behind = block, block
+    near, far = [], []
+    for step in range(1, n // 2 + 1):
+        ahead = lax.ppermute(ahead, axis, forward)
+        near.append(ahead)
+        if step < n - n // 2:
+            behind = lax.ppermute(behind, axis, backward)
+            far.append(behind)
+    return jnp.concatenate([block] + near + far[::-1], axis=1)
 
 
 def solution(mesh):

time: 202 us -> 225 us (1.11)
  the two profiles are of different devices: /device:TPU:193 before, /device:TPU:224 now
where the time goes in v2:
time: 225 us; the launch traced here: 220 us
  waiting for transfers between devices  104 us (46%)
  local copies, waits for them, and re-layouts  32.9 us (15%)
  Pallas kernels  32.8 us (15%)
  blocking collectives  21.2 us (9%)
  starting transfers between devices  13.8 us (6%)
  between operations  13.5 us (6%)
    ppermute x8, waiting for transfers between devices, ring_gather(): ahead = lax.ppermute(ahead, axis, forward)  104 us
    pallas_call x1, Pallas kernels, convolve(): pl.pallas_call(functools.partial(conv_kernel, per_energy, total), out_sha...  32.8 us
    unnamed x24, local copies, waits for them, and re-layouts  28.2 us
    all_to_all x1, blocking collectives, per_device(): lax.all_to_all(outgoing, 'cell', split_axis=3, concat_axis=3, tiled=True)  21.2 us
    ppermute x7, starting transfers between devices, ring_gather(): behind = lax.ppermute(behind, axis, backward)  8.05 us
    ppermute x8, starting transfers between devices, ring_gather(): ahead = lax.ppermute(ahead, axis, forward)  5.79 us
  transfers between devices with their start and end apart: 16, of which 7 were waited for; matrix products, arithmetic and copies ran while one was open for 16% of the time, Pallas kernels for 0%

profile of v2, /device:TPU:224, one launch (start us, length us, event | category | flops | bytes accessed | tf_op | source)
XLA Modules:
  0.0 220.2 jit_solution(6274630946081703179)
XLA Ops:
  8.2 1.8 copy.30
  9.9 1.3 gather_fusion
  12.2 21.2 %all_to_all.5 = bf16[4,6,2,16,1,512]{5,2,1,0,4,3:T(2,128)(2,1)S(1)} all-to-all(bf16[4,6,2,16,1,512]{5,2,1,0,4,3:T(2,128)(2,1)S(1)} %broadcast_select_fusion), channel_id=1, replica_groups=mesh['energy'=16,'cell'=16] {'cell'}, dimensions={3} | all-to-all | bytes 1572864 | tf_op jit(solution)/shard_map/all_to_all | solution.py:93
  33.9 28.2 %collective-permute-done = bf16[4,6,2,16,512]{4,3,2,1,0:T(8,128)(2,1)S(1)} collective-permute-done((bf16[4,6,2,16,512]{4,3,2,1,0:T(8,128)(2,1)S(1)}, bf16[4,6,2,16,512]{4,3,2,1,0:T(8,128)(2,1)S(1)}, u32[]{:S(2)}, u32[]{:S(2)}) %collective-permute-start) | collective-permute-done | bytes 786464 | tf_op jit(solution)/shard_map/ppermute | solution.py:109
  62.1 1.7 collective-permute-start.8
  63.8 26.5 %collective-permute-done.1 = bf16[4,6,2,16,512]{4,3,2,1,0:T(8,128)(2,1)S(1)} collective-permute-done((bf16[4,6,2,16,512]{4,3,2,1,0:T(8,128)(2,1)S(1)}, bf16[4,6,2,16,512]{4,3,2,1,0:T(8,128)(2,1)S(1)}, u32[]{:S(2)}, u32[]{:S(2)}) %collective-permute-start.1) | collective-permute-done | bytes 786464 | tf_op jit(solution)/shard_map/ppermute | solution.py:109
  90.3 1.8 collective-permute-start.9
  92.1 14.8 %collective-permute-done.2 = bf16[4,6,2,16,512]{4,3,2,1,0:T(8,128)(2,1)S(1)} collective-permute-done((bf16[4,6,2,16,512]{4,3,2,1,0:T(8,128)(2,1)S(1)}, bf16[4,6,2,16,512]{4,3,2,1,0:T(8,128)(2,1)S(1)}, u32[]{:S(2)}, u32[]{:S(2)}) %collective-permute-start.2) | collective-permute-done | bytes 786464 | tf_op jit(solution)/shard_map/ppermute | solution.py:109
  106.9 1.7 collective-permute-start.10
  108.6 9.8 %collective-permute-done.3 = bf16[4,6,2,16,512]{4,3,2,1,0:T(8,128)(2,1)} collective-permute-done((bf16[4,6,2,16,512]{4,3,2,1,0:T(8,128)(2,1)S(1)}, bf16[4,6,2,16,512]{4,3,2,1,0:T(8,128)(2,1)}, u32[]{:S(2)}, u32[]{:S(2)}) %collective-permute-start.3) | collective-permute-done | bytes 786464 | tf_op jit(solution)/shard_map/ppermute | solution.py:109
  118.4 1.7 collective-permute-start.11
  121.1 9.0 %collective-permute-done.4 = bf16[4,6,2,16,512]{4,3,2,1,0:T(8,128)(2,1)} collective-permute-done((bf16[4,6,2,16,512]{4,3,2,1,0:T(8,128)(2,1)}, bf16[4,6,2,16,512]{4,3,2,1,0:T(8,128)(2,1)}, u32[]{:S(2)}, u32[]{:S(2)}) %collective-permute-start.4) | collective-permute-done | bytes 786464 | tf_op jit(solution)/shard_map/ppermute | solution.py:109
  131.1 1.0 collective-permute-start.12
  132.6 9.2 %collective-permute-done.5 = bf16[4,6,2,16,512]{4,3,2,1,0:T(8,128)(2,1)} collective-permute-done((bf16[4,6,2,16,512]{4,3,2,1,0:T(8,128)(2,1)}, bf16[4,6,2,16,512]{4,3,2,1,0:T(8,128)(2,1)}, u32[]{:S(2)}, u32[]{:S(2)}) %collective-permute-start.5) | collective-permute-done | bytes 786464 | tf_op jit(solution)/shard_map/ppermute | solution.py:109
  141.8 1.9 collective-permute-start.6
  144.1 1.3 constant_dynamic-update-slice_fusion.15
  145.4 2.1 constant_dynamic-update-slice_fusion.14
  147.5 6.0 %collective-permute-done.6 = bf16[4,6,2,16,512]{4,3,2,1,0:T(8,128)(2,1)} collective-permute-done((bf16[4,6,2,16,512]{4,3,2,1,0:T(8,128)(2,1)}, bf16[4,6,2,16,512]{4,3,2,1,0:T(8,128)(2,1)}, u32[]{:S(2)}, u32[]{:S(2)}) %collective-permute-start.6) | collective-permute-done | bytes 786464 | tf_op jit(solution)/shard_map/ppermute | solution.py:109
  153.6 3.1 %collective-permute-start.7 = (bf16[4,6,2,16,512]{4,3,2,1,0:T(8,128)(2,1)}, bf16[4,6,2,16,512]{4,3,2,1,0:T(8,128)(2,1)S(1)}, u32[]{:S(2)}, u32[]{:S(2)}) collective-permute-start(bf16[4,6,2,16,512]{4,3,2,1,0:T(8,128)(2,1)} %collective-permute-done.6), channel_id=1, source_target_pairs={{0,16},{16,32},{32,48},{48,64},{64,80},{80,96},{96,112},{112,128},... | collective-permute-start | bytes 2359304 | tf_op jit(solution)/shard_map/ppermute | solution.py:109
  156.7 2.1 constant_dynamic-update-slice_fusion.13
  158.8 2.1 constant_dynamic-update-slice_fusion.12
  160.9 2.1 constant_dynamic-update-slice_fusion.11
  163.0 2.1 constant_dynamic-update-slice_fusion.10
  165.1 2.1 constant_dynamic-update-slice_fusion.9
  167.2 2.1 constant_dynamic-update-slice_fusion.8
  169.3 1.0 constant_dynamic-update-slice_fusion.7
  171.3 2.1 constant_dynamic-update-slice_fusion.5
  173.4 2.2 constant_dynamic-update-slice_fusion.4
  175.5 2.1 constant_dynamic-update-slice_fusion.3
  177.7 1.0 constant_dynamic-update-slice_fusion.2
  178.7 1.0 constant_dynamic-update-slice_fusion.1
  180.7 32.8 %shard_map.55 = f32[4,6,2,16,512]{4,3,2,1,0:T(8,128)} custom-call(s32[7]{0:T(128)S(1)} %pad_add_fusion.head_ref, s32[288]{0:T(512)S(1)} %reshape.184.lists_ref, s32[288]{0:T(512)S(1)} %fusion.3.places_ref, bf16[4,96,2,16,512]{4,3,2,1,0:T(8,128)(2,1)} %all-gather.2.cloned.1.call-done.g_ref, bf16[4,96,2,16,512]{4,3,2,1,0:T(8,128)(2,1)} %constant_dynamic-update-slice_fusion.w_ref), custom_call_target="tpu_custom_call" | custom-call | tf_op jit(solution)/shard_map/pallas_call | solution.py:72
  (56 shorter events, 7.8 us)
Async XLA Ops:
  6.5 113.6 %copy-start = (s32[16,16,3]{1,0,2:T(8,128)S(1)}, s32[16,16,3]{1,0,2:T(8,128)}, u32[]{:S(2)}) copy-start(s32[16,16,3]{1,0,2:T(8,128)} %param.8) | copy-start | bytes 9220
  6.5 174.1 %all-gather.2.cloned.1.call-start = ((), (), s32[]{:S(2)}) async-start(), calls=%async_computation.1 | async-start | bytes 13369344 | tf_op jit(solution)/shard_map/all_gather | solution.py:95
  33.8 28.2 %collective-permute-start = (bf16[4,6,2,16,512]{4,3,2,1,0:T(8,128)(2,1)S(1)}, bf16[4,6,2,16,512]{4,3,2,1,0:T(8,128)(2,1)S(1)}, u32[]{:S(2)}, u32[]{:S(2)}) collective-permute-start(bf16[4,6,2,16,512]{4,3,2,1,0:T(8,128)(2,1)S(1)} %bitcast.20), channel_id=1, source_target_pairs={{0,16},{16,32},{32,48},{48,64},{64,80},{80,96},{96,112},{112,128},... | collective-permute-start | bytes 2359304 | tf_op jit(solution)/shard_map/ppermute | solution.py:109
  62.1 28.2 %copy-start.3 = (bf16[4,6,2,16,512]{4,3,2,1,0:T(8,128)(2,1)}, bf16[4,6,2,16,512]{4,3,2,1,0:T(8,128)(2,1)S(1)}, u32[]{:S(2)}) copy-start(bf16[4,6,2,16,512]{4,3,2,1,0:T(8,128)(2,1)S(1)} %collective-permute-done) | copy-start | bytes 2359300
  62.1 28.2 %collective-permute-start.1 = (bf16[4,6,2,16,512]{4,3,2,1,0:T(8,128)(2,1)S(1)}, bf16[4,6,2,16,512]{4,3,2,1,0:T(8,128)(2,1)S(1)}, u32[]{:S(2)}, u32[]{:S(2)}) collective-permute-start(bf16[4,6,2,16,512]{4,3,2,1,0:T(8,128)(2,1)S(1)} %collective-permute-done), channel_id=1, source_target_pairs={{0,16},{16,32},{32,48},{48,64},{64,80},{80,96},{96,112},{112,128},... | collective-permute-start | bytes 2359304 | tf_op jit(solution)/shard_map/ppermute | solution.py:109
  62.1 28.2 %collective-permute-start.8 = (bf16[4,6,2,16,512]{4,3,2,1,0:T(8,128)(2,1)S(1)}, bf16[4,6,2,16,512]{4,3,2,1,0:T(8,128)(2,1)S(1)}, u32[]{:S(2)}, u32[]{:S(2)}) collective-permute-start(bf16[4,6,2,16,512]{4,3,2,1,0:T(8,128)(2,1)S(1)} %bitcast.21), channel_id=1, source_target_pairs={{0,240},{16,0},{32,16},{48,32},{64,48},{80,64},{96,80},{112,96},{1... | collective-permute-start | bytes 2359304 | tf_op jit(solution)/shard_map/ppermute | solution.py:112
  90.3 16.5 %copy-start.1 = (bf16[4,6,2,16,512]{4,3,2,1,0:T(8,128)(2,1)}, bf16[4,6,2,16,512]{4,3,2,1,0:T(8,128)(2,1)S(1)}, u32[]{:S(2)}) copy-start(bf16[4,6,2,16,512]{4,3,2,1,0:T(8,128)(2,1)S(1)} %collective-permute-done.1) | copy-start | bytes 2359300
  90.3 16.5 %collective-permute-start.2 = (bf16[4,6,2,16,512]{4,3,2,1,0:T(8,128)(2,1)S(1)}, bf16[4,6,2,16,512]{4,3,2,1,0:T(8,128)(2,1)S(1)}, u32[]{:S(2)}, u32[]{:S(2)}) collective-permute-start(bf16[4,6,2,16,512]{4,3,2,1,0:T(8,128)(2,1)S(1)} %collective-permute-done.1), channel_id=1, source_target_pairs={{0,16},{16,32},{32,48},{48,64},{64,80},{80,96},{96,112},{112,128},... | collective-permute-start | bytes 2359304 | tf_op jit(solution)/shard_map/ppermute | solution.py:109
  90.3 16.5 %collective-permute-start.9 = (bf16[4,6,2,16,512]{4,3,2,1,0:T(8,128)(2,1)S(1)}, bf16[4,6,2,16,512]{4,3,2,1,0:T(8,128)(2,1)S(1)}, u32[]{:S(2)}, u32[]{:S(2)}) collective-permute-start(bf16[4,6,2,16,512]{4,3,2,1,0:T(8,128)(2,1)S(1)} %collective-permute-done.8), channel_id=1, source_target_pairs={{0,240},{16,0},{32,16},{48,32},{64,48},{80,64},{96,80},{112,96},{1... | collective-permute-start | bytes 2359304 | tf_op jit(solution)/shard_map/ppermute | solution.py:112
  106.9 11.5 %copy-start.2 = (bf16[4,6,2,16,512]{4,3,2,1,0:T(8,128)(2,1)}, bf16[4,6,2,16,512]{4,3,2,1,0:T(8,128)(2,1)S(1)}, u32[]{:S(2)}) copy-start(bf16[4,6,2,16,512]{4,3,2,1,0:T(8,128)(2,1)S(1)} %collective-permute-done.2) | copy-start | bytes 2359300
  106.9 11.5 %collective-permute-start.3 = (bf16[4,6,2,16,512]{4,3,2,1,0:T(8,128)(2,1)S(1)}, bf16[4,6,2,16,512]{4,3,2,1,0:T(8,128)(2,1)}, u32[]{:S(2)}, u32[]{:S(2)}) collective-permute-start(bf16[4,6,2,16,512]{4,3,2,1,0:T(8,128)(2,1)S(1)} %collective-permute-done.2), channel_id=1, source_target_pairs={{0,16},{16,32},{32,48},{48,64},{64,80},{80,96},{96,112},{112,128},... | collective-permute-start | bytes 2359304 | tf_op jit(solution)/shard_map/ppermute | solution.py:109
  106.9 11.5 %collective-permute-start.10 = (bf16[4,6,2,16,512]{4,3,2,1,0:T(8,128)(2,1)S(1)}, bf16[4,6,2,16,512]{4,3,2,1,0:T(8,128)(2,1)S(1)}, u32[]{:S(2)}, u32[]{:S(2)}) collective-permute-start(bf16[4,6,2,16,512]{4,3,2,1,0:T(8,128)(2,1)S(1)} %collective-permute-done.9), channel_id=1, source_target_pairs={{0,240},{16,0},{32,16},{48,32},{64,48},{80,64},{96,80},{112,96},{1... | collective-permute-start | bytes 2359304 | tf_op jit(solution)/shard_map/ppermute | solution.py:112
  118.4 11.7 %collective-permute-start.4 = (bf16[4,6,2,16,512]{4,3,2,1,0:T(8,128)(2,1)}, bf16[4,6,2,16,512]{4,3,2,1,0:T(8,128)(2,1)}, u32[]{:S(2)}, u32[]{:S(2)}) collective-permute-start(bf16[4,6,2,16,512]{4,3,2,1,0:T(8,128)(2,1)} %collective-permute-done.3), channel_id=1, source_target_pairs={{0,16},{16,32},{32,48},{48,64},{64,80},{80,96},{96,112},{112,128},... | collective-permute-start | bytes 2359304 | tf_op jit(solution)/shard_map/ppermute | solution.py:109
  118.4 12.7 %collective-permute-start.11 = (bf16[4,6,2,16,512]{4,3,2,1,0:T(8,128)(2,1)S(1)}, bf16[4,6,2,16,512]{4,3,2,1,0:T(8,128)(2,1)}, u32[]{:S(2)}, u32[]{:S(2)}) collective-permute-start(bf16[4,6,2,16,512]{4,3,2,1,0:T(8,128)(2,1)S(1)} %collective-permute-done.10), channel_id=1, source_target_pairs={{0,240},{16,0},{32,16},{48,32},{64,48},{80,64},{96,80},{112,96},{1... | collective-permute-start | bytes 2359304 | tf_op jit(solution)/shard_map/ppermute | solution.py:112
  130.1 11.7 %collective-permute-start.5 = (bf16[4,6,2,16,512]{4,3,2,1,0:T(8,128)(2,1)}, bf16[4,6,2,16,512]{4,3,2,1,0:T(8,128)(2,1)}, u32[]{:S(2)}, u32[]{:S(2)}) collective-permute-start(bf16[4,6,2,16,512]{4,3,2,1,0:T(8,128)(2,1)} %collective-permute-done.4), channel_id=1, source_target_pairs={{0,16},{16,32},{32,48},{48,64},{64,80},{80,96},{96,112},{112,128},... | collective-permute-start | bytes 2359304 | tf_op jit(solution)/shard_map/ppermute | solution.py:109
  131.1 12.8 %collective-permute-start.12 = (bf16[4,6,2,16,512]{4,3,2,1,0:T(8,128)(2,1)}, bf16[4,6,2,16,512]{4,3,2,1,0:T(8,128)(2,1)}, u32[]{:S(2)}, u32[]{:S(2)}) collective-permute-start(bf16[4,6,2,16,512]{4,3,2,1,0:T(8,128)(2,1)} %collective-permute-done.11), channel_id=1, source_target_pairs={{0,240},{16,0},{32,16},{48,32},{64,48},{80,64},{96,80},{112,96},{1... | collective-permute-start | bytes 2359304 | tf_op jit(solution)/shard_map/ppermute | solution.py:112
  141.8 11.7 %collective-permute-start.6 = (bf16[4,6,2,16,512]{4,3,2,1,0:T(8,128)(2,1)}, bf16[4,6,2,16,512]{4,3,2,1,0:T(8,128)(2,1)}, u32[]{:S(2)}, u32[]{:S(2)}) collective-permute-start(bf16[4,6,2,16,512]{4,3,2,1,0:T(8,128)(2,1)} %collective-permute-done.5), channel_id=1, source_target_pairs={{0,16},{16,32},{32,48},{48,64},{64,80},{80,96},{96,112},{112,128},... | collective-permute-start | bytes 2359304 | tf_op jit(solution)/shard_map/ppermute | solution.py:109
  143.9 14.9 %collective-permute-start.13 = (bf16[4,6,2,16,512]{4,3,2,1,0:T(8,128)(2,1)}, bf16[4,6,2,16,512]{4,3,2,1,0:T(8,128)(2,1)}, u32[]{:S(2)}, u32[]{:S(2)}) collective-permute-start(bf16[4,6,2,16,512]{4,3,2,1,0:T(8,128)(2,1)} %collective-permute-done.12), channel_id=1, source_target_pairs={{0,240},{16,0},{32,16},{48,32},{64,48},{80,64},{96,80},{112,96},{1... | collective-permute-start | bytes 2359304 | tf_op jit(solution)/shard_map/ppermute | solution.py:112
  153.6 15.7 %collective-permute-start.7 = (bf16[4,6,2,16,512]{4,3,2,1,0:T(8,128)(2,1)}, bf16[4,6,2,16,512]{4,3,2,1,0:T(8,128)(2,1)S(1)}, u32[]{:S(2)}, u32[]{:S(2)}) collective-permute-start(bf16[4,6,2,16,512]{4,3,2,1,0:T(8,128)(2,1)} %collective-permute-done.6), channel_id=1, source_target_pairs={{0,16},{16,32},{32,48},{48,64},{64,80},{80,96},{96,112},{112,128},... | collective-permute-start | bytes 2359304 | tf_op jit(solution)/shard_map/ppermute | solution.py:109
  158.8 11.5 %collective-permute-start.14 = (bf16[4,6,2,16,512]{4,3,2,1,0:T(8,128)(2,1)}, bf16[4,6,2,16,512]{4,3,2,1,0:T(8,128)(2,1)S(1)}, u32[]{:S(2)}, u32[]{:S(2)}) collective-permute-start(bf16[4,6,2,16,512]{4,3,2,1,0:T(8,128)(2,1)} %collective-permute-done.13), channel_id=1, source_target_pairs={{0,240},{16,0},{32,16},{48,32},{64,48},{80,64},{96,80},{112,96},{1... | collective-permute-start | bytes 2359304 | tf_op jit(solution)/shard_map/ppermute | solution.py:112
Sparse Core Ops, SparseCore 0:
  9.2 93.6 all-gather.1

commit v3 on v1

--- a/solution.py
+++ b/solution.py
@@ -32,21 +32,23 @@
     return head, lists.reshape(-1).astype(jnp.int32)
 
 
-def conv_kernel(per_energy, total, head_ref, lists_ref, g_ref, w_ref, o_ref):
+def conv_kernel(per_energy, total, head_ref, lists_ref, x_ref, o_ref):
     base = head_ref[per_energy]
-    rows, width = g_ref.shape[2], g_ref.shape[3]
+    rows, width = x_ref.shape[4], x_ref.shape[5]
     for chunk in range(width // LANES):
         lanes = pl.ds(chunk * LANES, LANES)
         for e in range(per_energy):
             def body(t, acc, e=e, lanes=lanes):
                 w = lists_ref[e * total + t]
                 u = base + e - w
+                ug, uo = u // per_energy, u % per_energy
+                wg, wo = w // per_energy, w % per_energy
                 out = list(acc)
                 for kind in range(2):
-                    gr = g_ref[2 * kind, u, :, lanes].astype(jnp.float32)
-                    gi = g_ref[2 * kind + 1, u, :, lanes].astype(jnp.float32)
-                    wr = w_ref[2 * kind, w, :, lanes].astype(jnp.float32)
-                    wi = w_ref[2 * kind + 1, w, :, lanes].astype(jnp.float32)
+                    gr = x_ref[ug, 0, 2 * kind, uo, :, lanes].astype(jnp.float32)
+                    gi = x_ref[ug, 0, 2 * kind + 1, uo, :, lanes].astype(jnp.float32)
+                    wr = x_ref[wg, 1, 2 * kind, wo, :, lanes].astype(jnp.float32)
+                    wi = x_ref[wg, 1, 2 * kind + 1, wo, :, lanes].astype(jnp.float32)
                     out[2 * kind] = out[2 * kind] - (gr * wi + gi * wr)
                     out[2 * kind + 1] = out[2 * kind + 1] + (gr * wr - gi * wi)
                 return tuple(out)
@@ -57,11 +59,12 @@
                 o_ref[comp, e, :, lanes] = acc[comp] * SCALE
 
 
-def convolve(head, lists, whole, every, per_energy):
-    comps, energies, positions, rows, width = whole.shape
+def convolve(head, lists, stacked, per_energy):
+    groups, pair, comps, _, positions, rows, width = stacked.shape
     total = lists.shape[0] // per_energy
     in_block = pl.BlockSpec(
-        (comps, energies, pl.squeezed, rows, width), lambda p, h, l: (0, 0, p, 0, 0)
+        (groups, pair, comps, per_energy, pl.squeezed, rows, width),
+        lambda p, h, l: (0, 0, 0, 0, p, 0, 0),
     )
     out_block = pl.BlockSpec(
         (comps, per_energy, pl.squeezed, rows, width), lambda p, h, l: (0, 0, p, 0, 0)
@@ -72,11 +75,11 @@
         grid_spec=pltpu.PrefetchScalarGridSpec(
             num_scalar_prefetch=2,
             grid=(positions,),
-            in_specs=[in_block, in_block],
+            in_specs=[in_block],
             out_specs=out_block,
         ),
         compiler_params=pltpu.CompilerParams(vmem_limit_bytes=48 * 1024 * 1024),
-    )(head, lists, whole, every)
+    )(head, lists, stacked)
 
 
 def per_device(green, screened, cell_map, shift_table, shift_count):
@@ -89,11 +92,94 @@
     outgoing = outgoing.reshape(4, per_energy, per_cell, cell_count, screened.shape[3], width)
     arrived = lax.all_to_all(outgoing, "cell", split_axis=3, concat_axis=3, tiled=True)
     owned = arrived.reshape(4, per_energy, per_cell, green.shape[3], width)
-    whole = lax.all_gather(green, "energy", axis=1, tiled=True)
-    every = lax.all_gather(owned, "energy", axis=1, tiled=True)
+    stacked = gather_energy(jnp.stack([green, owned]))
     group = lax.axis_index("energy")
     head, lists = term_lists(shift_table, shift_count, group, per_energy)
-    return convolve(head, lists, whole, every, per_energy)
+    return convolve(head, lists, stacked, per_energy)
+
+
+def gather_kernel(chips, x_ref, out_ref, local_sem, ring_send, ring_recv, pass_send, pass_recv):
+    me = lax.axis_index("energy")
+    cell = lax.axis_index("cell")
+    chip, core = me // 2, me % 2
+    step_dir = 1 - 2 * core
+    partner = me + step_dir
+    ahead = 2 * ((chip + step_dir + chips) % chips) + core
+
+    def origin(k):
+        return 2 * ((chip - step_dir * k + chips) % chips) + core
+
+    def ring_copy(k):
+        slot = origin(k - 1)
+        src = x_ref if k == 1 else out_ref.at[slot]
+        return pltpu.make_async_remote_copy(
+            src_ref=src, dst_ref=out_ref.at[slot],
+            send_sem=ring_send.at[k], recv_sem=ring_recv.at[k],
+            device_id=(ahead, cell), device_id_type=pl.DeviceIdType.MESH,
+        )
+
+    def pass_copy(k):
+        slot = origin(k)
+        src = x_ref if k == 0 else out_ref.at[slot]
+        return pltpu.make_async_remote_copy(
+            src_ref=src, dst_ref=out_ref.at[slot],
+            send_sem=pass_send.at[k], recv_sem=pass_recv.at[k],
+            device_id=(partner, cell), device_id_type=pl.DeviceIdType.MESH,
+        )
+
+    def arrival(k):
+        slot = origin(k)
+        return pltpu.make_async_remote_copy(
+            src_ref=out_ref.at[slot], dst_ref=out_ref.at[slot],
+            send_sem=ring_send.at[k], recv_sem=ring_recv.at[k],
+            device_id=(ahead, cell), device_id_type=pl.DeviceIdType.MESH,
+        )
+
+    def handed(k):
+        slot = 2 * ((chip + step_dir * k + chips) % chips) + 1 - core
+        return pltpu.make_async_remote_copy(
+            src_ref=out_ref.at[slot], dst_ref=out_ref.at[slot],
+            send_sem=pass_send.at[k], recv_sem=pass_recv.at[k],
+            device_id=(partner, cell), device_id_type=pl.DeviceIdType.MESH,
+        )
+
+    local = pltpu.make_async_copy(x_ref, out_ref.at[me], local_sem)
+    local.start()
+    sends = [ring_copy(1), pass_copy(0)]
+    for copy in sends:
+        copy.start()
+    for k in range(1, chips):
+        arrival(k).wait_recv()
+        onward = [pass_copy(k)]
+        if k + 1 < chips:
+            onward.append(ring_copy(k + 1))
+        for copy in onward:
+            copy.start()
+        sends.extend(onward)
+    for k in range(chips):
+        handed(k).wait_recv()
+    for copy in sends:
+        copy.wait_send()
+    local.wait()
+
+
+def gather_energy(block):
+    groups = lax.axis_size("energy")
+    chips = groups // 2
+    return pl.pallas_call(
+        functools.partial(gather_kernel, chips),
+        out_shape=jax.ShapeDtypeStruct((groups,) + block.shape, block.dtype),
+        in_specs=[pl.BlockSpec(memory_space=pl.ANY)],
+        out_specs=pl.BlockSpec(memory_space=pl.ANY),
+        scratch_shapes=[
+            pltpu.SemaphoreType.DMA(()),
+            pltpu.SemaphoreType.DMA((chips,)),
+            pltpu.SemaphoreType.DMA((chips,)),
+            pltpu.SemaphoreType.DMA((chips,)),
+            pltpu.SemaphoreType.DMA((chips,)),
+        ],
+        compiler_params=pltpu.CompilerParams(has_side_effects=True),
+    )(block)
 
 
 def solution(mesh):

time: 202 us -> 223 us (1.10)
  the two profiles are of different devices: /device:TPU:193 before, /device:TPU:224 now
where the time goes in v3:
time: 223 us
  Pallas kernels  193 us (87%)
  waiting for transfers between devices  12.5 us (6%)
  starting transfers between devices  7.17 us (3%)
  local copies, waits for them, and re-layouts  5.58 us (3%)
  other arithmetic  3.89 us (2%)
    pallas_call x1, Pallas kernels, gather_energy(): pl.pallas_call(functools.partial(gather_kernel, chips), out_shape=jax.Sha...  148 us
    pallas_call x1, Pallas kernels, convolve(): pl.pallas_call(functools.partial(conv_kernel, per_energy, total), out_sha...  45.1 us
    all_to_all x1, waiting for transfers between devices, per_device(): lax.all_to_all(outgoing, 'cell', split_axis=3, concat_axis=3, tiled=True)  12.5 us
    all_to_all x1, starting transfers between devices, per_device(): lax.all_to_all(outgoing, 'cell', split_axis=3, concat_axis=3, tiled=True)  7.17 us
  transfers between devices with their start and end apart: 1, of which 1 were waited for; matrix products, arithmetic and copies ran while one was open for 1% of the time, Pallas kernels for 0%

profile of v3, /device:TPU:224, one launch (start us, length us, event | category | flops | bytes accessed | tf_op | source)
XLA Modules:
  0.0 222.5 jit_solution(3354950784095325559)
XLA Ops:
  0.0 0.0 copy-start
  0.0 0.7 reshape.180
  0.8 0.1 copy.21
  0.8 0.1 reshape.181
  0.9 1.7 copy.28
  2.7 1.3 gather_fusion
  4.0 1.9 broadcast_select_fusion
  5.8 0.0 copy-start.1
  5.8 7.2 %all-to-all-start = ((bf16[4,6,2,16,1,512]{5,2,1,0,4,3:T(2,128)(2,1)}), bf16[4,6,2,16,1,512]{5,2,1,0,4,3:T(2,128)(2,1)S(1)}, u32[]{:S(2)}, u32[]{:S(2)}) async-start(bf16[4,6,2,16,1,512]{5,2,1,0,4,3:T(2,128)(2,1)} %broadcast_select_fusion), calls=%async_computation | async-start | bytes 1572864 | tf_op jit(solution)/shard_map/all_to_all | solution.py:93
  13.0 0.7 dynamic-slice_bitcast_fusion
  13.7 0.0 copy-done
  13.7 0.1 iota_compare_fusion.1
  13.8 0.1 lt.47
  13.9 0.1 copy.19
  14.0 0.1 squeeze.3
  14.1 0.1 iota.28
  14.2 0.1 iota.29
  14.3 0.1 fusion.2
  14.3 0.2 reduce_window_sum.11
  14.6 0.2 select_reduce_fusion
  14.7 0.1 reshape.179.lists_ref
  14.8 0.1 convert_reduce_fusion
  14.9 0.1 pad_add_fusion.head_ref
  15.0 12.5 %all-to-all-done = bf16[4,6,2,16,1,512]{5,2,1,0,4,3:T(2,128)(2,1)S(1)} async-done(((bf16[4,6,2,16,1,512]{5,2,1,0,4,3:T(2,128)(2,1)}), bf16[4,6,2,16,1,512]{5,2,1,0,4,3:T(2,128)(2,1)S(1)}, u32[]{:S(2)}, u32[]{:S(2)}) %all-to-all-start) | async-done | bytes 786464 | tf_op jit(solution)/shard_map/all_to_all | solution.py:93
  27.5 0.4 copy.27
  27.9 0.0 copy-done.1
  27.9 1.3 pad_maximum_fusion.x_ref
  29.2 148.2 %shard_map.55.x_ref = bf16[16,2,4,6,2,16,512]{6,5,4,3,2,1,0:T(8,128)(2,1)} custom-call(bf16[2,4,6,2,16,512]{5,4,3,2,1,0:T(8,128)(2,1)} %pad_maximum_fusion.x_ref), custom_call_target="tpu_custom_call" | custom-call | tf_op jit(solution)/shard_map/pallas_call | solution.py:169
  177.4 45.1 %shard_map.56 = f32[4,6,2,16,512]{4,3,2,1,0:T(8,128)} custom-call(s32[7]{0:T(128)S(1)} %pad_add_fusion.head_ref, s32[288]{0:T(512)S(1)} %reshape.179.lists_ref, bf16[16,2,4,6,2,16,512]{6,5,4,3,2,1,0:T(8,128)(2,1)} %shard_map.55.x_ref), custom_call_target="tpu_custom_call" | custom-call | tf_op jit(solution)/shard_map/pallas_call | solution.py:72
  (8 shorter events, 0.1 us)
Async XLA Ops:
  0.0 13.7 %copy-start = (s32[16,16,3]{1,0,2:T(8,128)S(1)}, s32[16,16,3]{1,0,2:T(8,128)}, u32[]{:S(2)}) copy-start(s32[16,16,3]{1,0,2:T(8,128)} %param.8) | copy-start | bytes 9220
  5.8 22.1 %copy-start.1 = (bf16[4,6,2,16,512]{4,3,2,1,0:T(8,128)(2,1)S(1)}, bf16[4,6,2,16,512]{4,3,2,1,0:T(8,128)(2,1)}, u32[]{:S(2)}) copy-start(bf16[4,6,2,16,512]{4,3,2,1,0:T(8,128)(2,1)} %param.5) | copy-start | bytes 2359300
  5.8 21.7 %all-to-all-start = ((bf16[4,6,2,16,1,512]{5,2,1,0,4,3:T(2,128)(2,1)}), bf16[4,6,2,16,1,512]{5,2,1,0,4,3:T(2,128)(2,1)S(1)}, u32[]{:S(2)}, u32[]{:S(2)}) async-start(bf16[4,6,2,16,1,512]{5,2,1,0,4,3:T(2,128)(2,1)} %broadcast_select_fusion), calls=%async_computation | async-start | bytes 1572864 | tf_op jit(solution)/shard_map/all_to_all | solution.py:93

commit v4 on v1

--- a/solution.py
+++ b/solution.py
@@ -32,28 +32,39 @@
     return head, lists.reshape(-1).astype(jnp.int32)
 
 
-def conv_kernel(per_energy, total, head_ref, lists_ref, g_ref, w_ref, o_ref):
+def conv_kernel(per_energy, total, head_ref, lists_ref, g_ref, w_ref, o_ref, gf, wf):
     base = head_ref[per_energy]
     rows, width = g_ref.shape[2], g_ref.shape[3]
+    comps = g_ref.shape[0]
+    held = base // per_energy + 1
     for chunk in range(width // LANES):
         lanes = pl.ds(chunk * LANES, LANES)
+
+        def widen(grp, carry, lanes=lanes):
+            energies = pl.ds(grp * per_energy, per_energy)
+            for comp in range(comps):
+                gf[comp, energies] = g_ref[comp, energies, :, lanes].astype(jnp.float32)
+                wf[comp, energies] = w_ref[comp, energies, :, lanes].astype(jnp.float32)
+            return carry
+
+        lax.fori_loop(0, held, widen, 0)
         for e in range(per_energy):
-            def body(t, acc, e=e, lanes=lanes):
+            def body(t, acc, e=e):
                 w = lists_ref[e * total + t]
                 u = base + e - w
                 out = list(acc)
                 for kind in range(2):
-                    gr = g_ref[2 * kind, u, :, lanes].astype(jnp.float32)
-                    gi = g_ref[2 * kind + 1, u, :, lanes].astype(jnp.float32)
-                    wr = w_ref[2 * kind, w, :, lanes].astype(jnp.float32)
-                    wi = w_ref[2 * kind + 1, w, :, lanes].astype(jnp.float32)
+                    gr = gf[2 * kind, u]
+                    gi = gf[2 * kind + 1, u]
+                    wr = wf[2 * kind, w]
+                    wi = wf[2 * kind + 1, w]
                     out[2 * kind] = out[2 * kind] - (gr * wi + gi * wr)
                     out[2 * kind + 1] = out[2 * kind + 1] + (gr * wr - gi * wi)
                 return tuple(out)
 
             zero = jnp.zeros((rows, LANES), jnp.float32)
             acc = lax.fori_loop(0, head_ref[e], body, (zero,) * 4)
-            for comp in range(4):
+            for comp in range(comps):
                 o_ref[comp, e, :, lanes] = acc[comp] * SCALE
 
 
@@ -74,6 +85,10 @@
             grid=(positions,),
             in_specs=[in_block, in_block],
             out_specs=out_block,
+            scratch_shapes=[
+                pltpu.VMEM((comps, energies, rows, LANES), jnp.float32),
+                pltpu.VMEM((comps, energies, rows, LANES), jnp.float32),
+            ],
         ),
         compiler_params=pltpu.CompilerParams(vmem_limit_bytes=48 * 1024 * 1024),
     )(head, lists, whole, every)

time: 202 us -> 198 us (0.980)
  the two profiles are of different devices: /device:TPU:193 before, /device:TPU:225 now
where the time goes in v4:
time: 198 us
  waiting for transfers between devices  125 us (63%)
  Pallas kernels  31.2 us (16%)
  blocking collectives  20.1 us (10%)
  between operations  13.5 us (7%)
  local copies, waits for them, and re-layouts  6.46 us (3%)
    all_gather x1, waiting for transfers between devices, per_device(): every = lax.all_gather(owned, 'energy', axis=1, tiled=True)  76.1 us
    all_gather x1, waiting for transfers between devices, per_device(): whole = lax.all_gather(green, 'energy', axis=1, tiled=True)  48.1 us
    pallas_call x1, Pallas kernels, convolve(): pl.pallas_call(functools.partial(conv_kernel, per_energy, total), out_sha...  31.2 us
    all_to_all x1, blocking collectives, per_device(): lax.all_to_all(outgoing, 'cell', split_axis=3, concat_axis=3, tiled=True)  20.1 us
  transfers between devices with their start and end apart: 2, of which 2 were waited for; matrix products, arithmetic and copies ran while one was open for 4% of the time, Pallas kernels for 0%

profile of v4, /device:TPU:225, one launch (start us, length us, event | category | flops | bytes accessed | tf_op | source)
XLA Modules:
  0.0 197.9 jit_solution(2702638712295125252)
XLA Ops:
  6.5 0.0 copy-start
  6.5 0.0 all-gather.4.cloned.1.call-start
  6.5 0.7 all-gather.4.cloned.1.call-update
  7.3 0.0 all-gather.6.cloned.1.call-start
  7.3 0.7 reshape.183
  8.0 0.1 copy.21
  8.1 0.1 reshape.184
  8.2 1.8 copy.26
  10.0 1.3 gather_fusion
  11.3 1.0 broadcast_select_fusion
  12.3 20.1 %all_to_all.5 = bf16[4,6,2,16,1,512]{5,2,1,0,4,3:T(2,128)(2,1)S(1)} all-to-all(bf16[4,6,2,16,1,512]{5,2,1,0,4,3:T(2,128)(2,1)S(1)} %broadcast_select_fusion), channel_id=1, replica_groups=mesh['energy'=16,'cell'=16] {'cell'}, dimensions={3} | all-to-all | bytes 1572864 | tf_op jit(solution)/shard_map/all_to_all | solution.py:105
  32.3 1.3 copy.23
  33.6 0.0 all-gather.6.cloned.1.call-update
  33.7 0.7 dynamic-slice_bitcast_fusion
  34.4 0.1 iota_compare_fusion.1
  34.4 0.1 lt.47
  34.5 0.0 copy-done
  34.6 0.1 copy.19
  34.7 0.1 squeeze.3
  34.8 0.1 iota.28
  34.8 0.1 iota.29
  34.9 0.1 fusion.2
  35.0 0.2 reduce_window_sum.11
  35.2 0.2 select_reduce_fusion
  35.4 0.1 reshape.182.lists_ref
  35.5 0.1 convert_reduce_fusion
  35.6 0.1 pad_add_fusion.head_ref
  35.7 48.1 %all-gather.4.cloned.1.call-done.g_ref = bf16[4,96,2,16,512]{4,3,2,1,0:T(8,128)(2,1)} async-done(((bf16[4,6,2,16,512]{4,3,2,1,0:T(8,128)(2,1)}), bf16[4,96,2,16,512]{4,3,2,1,0:T(8,128)(2,1)}) %all-gather.4.cloned.1.call-update) | async-done | bytes 12582928 | tf_op jit(solution)/shard_map/all_gather | solution.py:107
  83.8 76.1 %all-gather.6.cloned.1.call-done = bf16[4,96,2,16,1,512]{5,3,2,1,0,4:T(8,128)(2,1)} async-done(((bf16[4,6,2,16,1,512]{5,3,2,1,0,4:T(8,128)(2,1)}), bf16[4,96,2,16,1,512]{5,3,2,1,0,4:T(8,128)(2,1)}) %all-gather.6.cloned.1.call-update) | async-done | bytes 12582928 | tf_op jit(solution)/shard_map/all_gather | solution.py:108
  159.9 31.2 %shard_map.55 = f32[4,6,2,16,512]{4,3,2,1,0:T(8,128)} custom-call(s32[7]{0:T(128)S(1)} %pad_add_fusion.head_ref, s32[288]{0:T(512)S(1)} %reshape.182.lists_ref, bf16[4,96,2,16,512]{4,3,2,1,0:T(8,128)(2,1)} %all-gather.4.cloned.1.call-done.g_ref, bf16[4,96,2,16,512]{4,3,2,1,0:T(8,128)(2,1)} %bitcast.14), custom_call_target="tpu_custom_call" | custom-call | tf_op jit(solution)/shard_map/pallas_call | solution.py:80
  (8 shorter events, 0.1 us)
Async XLA Ops:
  6.5 28.0 %copy-start = (s32[16,16,3]{1,0,2:T(8,128)S(1)}, s32[16,16,3]{1,0,2:T(8,128)}, u32[]{:S(2)}) copy-start(s32[16,16,3]{1,0,2:T(8,128)} %param.8) | copy-start | bytes 9220
  6.5 77.3 %all-gather.4.cloned.1.call-start = ((), (), s32[]{:S(2)}) async-start(), calls=%async_computation.1 | async-start | bytes 13369344 | tf_op jit(solution)/shard_map/all_gather | solution.py:107
  7.3 152.6 %all-gather.6.cloned.1.call-start = ((), (), s32[]{:S(2)}) async-start(), calls=%async_computation.2 | async-start | bytes 13369344 | tf_op jit(solution)/shard_map/all_gather | solution.py:108
Sparse Core Ops, SparseCore 0:
  9.2 74.5 all-gather.3
  85.7 74.1 all-gather.5

commit v5 on v1

--- a/solution.py
+++ b/solution.py
@@ -9,6 +9,7 @@
 
 SCALE = 0.2
 LANES = 128
+CHUNK = 128
 
 
 def term_lists(shift_table, shift_count, group, per_energy):
@@ -89,11 +90,15 @@
     outgoing = outgoing.reshape(4, per_energy, per_cell, cell_count, screened.shape[3], width)
     arrived = lax.all_to_all(outgoing, "cell", split_axis=3, concat_axis=3, tiled=True)
     owned = arrived.reshape(4, per_energy, per_cell, green.shape[3], width)
-    whole = lax.all_gather(green, "energy", axis=1, tiled=True)
-    every = lax.all_gather(owned, "energy", axis=1, tiled=True)
     group = lax.axis_index("energy")
     head, lists = term_lists(shift_table, shift_count, group, per_energy)
-    return convolve(head, lists, whole, every, per_energy)
+    parts = []
+    for start in range(0, width, CHUNK):
+        lanes = slice(start, start + CHUNK)
+        whole = lax.all_gather(green[..., lanes], "energy", axis=1, tiled=True)
+        every = lax.all_gather(owned[..., lanes], "energy", axis=1, tiled=True)
+        parts.append(convolve(head, lists, whole, every, per_energy))
+    return jnp.concatenate(parts, axis=-1)
 
 
 def solution(mesh):

time: 202 us -> 359 us (1.78)
  the two profiles are of different devices: /device:TPU:193 before, /device:TPU:224 now
where the time goes in v5:
time: 359 us; the launch traced here: 357 us
  waiting for transfers between devices  273 us (76%)
  Pallas kernels  28.9 us (8%)
  blocking collectives  21.2 us (6%)
  local copies, waits for them, and re-layouts  16.3 us (5%)
  between operations  13.6 us (4%)
    all_gather x4, waiting for transfers between devices, per_device(): every = lax.all_gather(owned[..., lanes], 'energy', axis=1, tiled=True)  166 us
    all_gather x4, waiting for transfers between devices, per_device(): whole = lax.all_gather(green[..., lanes], 'energy', axis=1, tiled=True)  104 us
    pallas_call x4, Pallas kernels, convolve(): pl.pallas_call(functools.partial(conv_kernel, per_energy, total), out_sha...  28.9 us
    all_to_all x1, blocking collectives, per_device(): lax.all_to_all(outgoing, 'cell', split_axis=3, concat_axis=3, tiled=True)  21.2 us
    unnamed x11, local copies, waits for them, and re-layouts  9.32 us
  transfers between devices with their start and end apart: 8, of which 8 were waited for; matrix products, arithmetic and copies ran while one was open for 2% of the time, Pallas kernels for 6%

profile of v5, /device:TPU:224, one launch (start us, length us, event | category | flops | bytes accessed | tf_op | source)
XLA Modules:
  0.0 356.7 jit_solution(16342397313978198971)
XLA Ops:
  6.5 2.2 fusion.4
  8.8 0.7 reshape.183
  9.7 1.8 copy.28
  11.5 1.3 gather_fusion
  12.7 1.0 broadcast_select_fusion
  13.7 21.2 %all_to_all.5 = bf16[4,6,2,16,1,512]{5,2,1,0,4,3:T(2,128)(2,1)S(1)} all-to-all(bf16[4,6,2,16,1,512]{5,2,1,0,4,3:T(2,128)(2,1)S(1)} %broadcast_select_fusion), channel_id=1, replica_groups=mesh['energy'=16,'cell'=16] {'cell'}, dimensions={3} | all-to-all | bytes 1572864 | tf_op jit(solution)/shard_map/all_to_all | solution.py:91
  34.9 0.4 copy.27
  35.3 1.0 fusion.3
  36.4 0.7 all-gather.13.cloned.1.call-update
  37.1 0.5 all-gather.15.cloned.1.call-update
  37.7 0.5 all-gather.17.cloned.1.call-update
  38.3 0.5 all-gather.19.cloned.1.call-update
  38.9 0.7 all-gather.21.cloned.1.call-update
  39.6 0.7 all-gather.23.cloned.1.call-update
  40.7 0.7 dynamic-slice_bitcast_fusion
  42.3 6.9 %all-gather.9.cloned.1.call-done.g_ref = bf16[4,96,2,16,128]{4,3,2,1,0:T(8,128)(2,1)} async-done(((bf16[4,6,2,16,128]{4,3,2,1,0:T(8,128)(2,1)}), bf16[4,96,2,16,128]{4,3,2,1,0:T(8,128)(2,1)}) %all-gather.9.cloned.1.call-update) | async-done | bytes 3145744 | tf_op jit(solution)/shard_map/all_gather | solution.py:98
  49.2 41.6 %all-gather.11.cloned.1.call-done.w_ref = bf16[4,96,2,16,128]{4,3,2,1,0:T(8,128)(2,1)} async-done(((bf16[4,6,2,16,128]{4,3,2,1,0:T(8,128)(2,1)}), bf16[4,96,2,16,128]{4,3,2,1,0:T(8,128)(2,1)}) %all-gather.11.cloned.1.call-update) | async-done | bytes 3145744 | tf_op jit(solution)/shard_map/all_gather | solution.py:99
  90.8 1.9 copy-done.1
  92.7 7.2 %shard_map.55 = f32[4,6,2,16,128]{4,3,2,1,0:T(8,128)S(1)} custom-call(s32[7]{0:T(128)S(1)} %pad_add_fusion.head_ref, s32[288]{0:T(512)S(1)} %reshape.182.lists_ref, bf16[4,96,2,16,128]{4,3,2,1,0:T(8,128)(2,1)S(1)} %copy-done.1, bf16[4,96,2,16,128]{4,3,2,1,0:T(8,128)(2,1)} %all-gather.11.cloned.1.call-done.w_ref), custom_call_target="tpu_custom_call" | custom-call | tf_op jit(solution)/shard_map/pallas_call | solution.py:70
  99.9 32.4 %all-gather.13.cloned.1.call-done.g_ref = bf16[4,96,2,16,128]{4,3,2,1,0:T(8,128)(2,1)} async-done(((bf16[4,6,2,16,128]{4,3,2,1,0:T(8,128)(2,1)}), bf16[4,96,2,16,128]{4,3,2,1,0:T(8,128)(2,1)}) %all-gather.13.cloned.1.call-update) | async-done | bytes 3145744 | tf_op jit(solution)/shard_map/all_gather | solution.py:98
  132.3 41.4 %all-gather.15.cloned.1.call-done.w_ref = bf16[4,96,2,16,128]{4,3,2,1,0:T(8,128)(2,1)} async-done(((bf16[4,6,2,16,128]{4,3,2,1,0:T(8,128)(2,1)}), bf16[4,96,2,16,128]{4,3,2,1,0:T(8,128)(2,1)}) %all-gather.15.cloned.1.call-update) | async-done | bytes 3145744 | tf_op jit(solution)/shard_map/all_gather | solution.py:99
  173.7 1.9 copy-done.2
  175.6 7.2 %shard_map.56 = f32[4,6,2,16,128]{4,3,2,1,0:T(8,128)S(1)} custom-call(s32[7]{0:T(128)S(1)} %pad_add_fusion.head_ref, s32[288]{0:T(512)S(1)} %reshape.182.lists_ref, bf16[4,96,2,16,128]{4,3,2,1,0:T(8,128)(2,1)S(1)} %copy-done.2, bf16[4,96,2,16,128]{4,3,2,1,0:T(8,128)(2,1)} %all-gather.15.cloned.1.call-done.w_ref), custom_call_target="tpu_custom_call" | custom-call | tf_op jit(solution)/shard_map/pallas_call | solution.py:70
  182.8 32.2 %all-gather.17.cloned.1.call-done.g_ref = bf16[4,96,2,16,128]{4,3,2,1,0:T(8,128)(2,1)} async-done(((bf16[4,6,2,16,128]{4,3,2,1,0:T(8,128)(2,1)}), bf16[4,96,2,16,128]{4,3,2,1,0:T(8,128)(2,1)}) %all-gather.17.cloned.1.call-update) | async-done | bytes 3145744 | tf_op jit(solution)/shard_map/all_gather | solution.py:98
  215.0 41.4 %all-gather.19.cloned.1.call-done.w_ref = bf16[4,96,2,16,128]{4,3,2,1,0:T(8,128)(2,1)} async-done(((bf16[4,6,2,16,128]{4,3,2,1,0:T(8,128)(2,1)}), bf16[4,96,2,16,128]{4,3,2,1,0:T(8,128)(2,1)}) %all-gather.19.cloned.1.call-update) | async-done | bytes 3145744 | tf_op jit(solution)/shard_map/all_gather | solution.py:99
  256.4 1.9 copy-done.3
  258.3 7.2 %shard_map.57 = f32[4,6,2,16,128]{4,3,2,1,0:T(8,128)S(1)} custom-call(s32[7]{0:T(128)S(1)} %pad_add_fusion.head_ref, s32[288]{0:T(512)S(1)} %reshape.182.lists_ref, bf16[4,96,2,16,128]{4,3,2,1,0:T(8,128)(2,1)S(1)} %copy-done.3, bf16[4,96,2,16,128]{4,3,2,1,0:T(8,128)(2,1)} %all-gather.19.cloned.1.call-done.w_ref), custom_call_target="tpu_custom_call" | custom-call | tf_op jit(solution)/shard_map/pallas_call | solution.py:70
  265.5 32.4 %all-gather.21.cloned.1.call-done.g_ref = bf16[4,96,2,16,128]{4,3,2,1,0:T(8,128)(2,1)} async-done(((bf16[4,6,2,16,128]{4,3,2,1,0:T(8,128)(2,1)}), bf16[4,96,2,16,128]{4,3,2,1,0:T(8,128)(2,1)}) %all-gather.21.cloned.1.call-update) | async-done | bytes 3145744 | tf_op jit(solution)/shard_map/all_gather | solution.py:98
  297.9 41.5 %all-gather.23.cloned.1.call-done.w_ref = bf16[4,96,2,16,128]{4,3,2,1,0:T(8,128)(2,1)} async-done(((bf16[4,6,2,16,128]{4,3,2,1,0:T(8,128)(2,1)}), bf16[4,96,2,16,128]{4,3,2,1,0:T(8,128)(2,1)}) %all-gather.23.cloned.1.call-update) | async-done | bytes 3145744 | tf_op jit(solution)/shard_map/all_gather | solution.py:99
  339.4 1.9 copy-done.4
  341.3 7.2 %shard_map.58 = f32[4,6,2,16,128]{4,3,2,1,0:T(8,128)S(1)} custom-call(s32[7]{0:T(128)S(1)} %pad_add_fusion.head_ref, s32[288]{0:T(512)S(1)} %reshape.182.lists_ref, bf16[4,96,2,16,128]{4,3,2,1,0:T(8,128)(2,1)S(1)} %copy-done.4, bf16[4,96,2,16,128]{4,3,2,1,0:T(8,128)(2,1)} %all-gather.23.cloned.1.call-done.w_ref), custom_call_target="tpu_custom_call" | custom-call | tf_op jit(solution)/shard_map/pallas_call | solution.py:70
  348.5 1.3 pad_maximum_fusion
  (38 shorter events, 1.7 us)
Async XLA Ops:
  6.5 33.8 %copy-start = (s32[16,16,3]{1,0,2:T(8,128)S(1)}, s32[16,16,3]{1,0,2:T(8,128)}, u32[]{:S(2)}) copy-start(s32[16,16,3]{1,0,2:T(8,128)} %param.8) | copy-start | bytes 9220
  6.5 42.7 %all-gather.9.cloned.1.call-start = ((), (), s32[]{:S(2)}) async-start(), calls=%async_computation.1 | async-start | bytes 3342336 | tf_op jit(solution)/shard_map/all_gather | solution.py:98
  8.7 82.1 %all-gather.11.cloned.1.call-start = ((), (), s32[]{:S(2)}) async-start(), calls=%async_computation.2 | async-start | bytes 3342336 | tf_op jit(solution)/shard_map/all_gather | solution.py:99
  36.4 96.0 %all-gather.13.cloned.1.call-start = ((), (), s32[]{:S(2)}) async-start(), calls=%async_computation.3 | async-start | bytes 3342336 | tf_op jit(solution)/shard_map/all_gather | solution.py:98
  37.1 136.6 %all-gather.15.cloned.1.call-start = ((), (), s32[]{:S(2)}) async-start(), calls=%async_computation.4 | async-start | bytes 3342336 | tf_op jit(solution)/shard_map/all_gather | solution.py:99
  37.7 177.4 %all-gather.17.cloned.1.call-start = ((), (), s32[]{:S(2)}) async-start(), calls=%async_computation.5 | async-start | bytes 3342336 | tf_op jit(solution)/shard_map/all_gather | solution.py:98
  38.3 218.2 %all-gather.19.cloned.1.call-start = ((), (), s32[]{:S(2)}) async-start(), calls=%async_computation.6 | async-start | bytes 3342336 | tf_op jit(solution)/shard_map/all_gather | solution.py:99
  38.8 259.1 %all-gather.21.cloned.1.call-start = ((), (), s32[]{:S(2)}) async-start(), calls=%async_computation.7 | async-start | bytes 3342336 | tf_op jit(solution)/shard_map/all_gather | solution.py:98
  39.6 299.8 %all-gather.23.cloned.1.call-start = ((), (), s32[]{:S(2)}) async-start(), calls=%async_computation.8 | async-start | bytes 3342336 | tf_op jit(solution)/shard_map/all_gather | solution.py:99
  90.8 1.9 copy-start.1
  173.7 1.9 copy-start.2
  256.4 1.9 copy-start.3
  339.4 1.9 copy-start.4
Sparse Core Ops, SparseCore 0:
  9.2 39.9 all-gather.8
  51.1 39.6 all-gather.10
  92.7 39.6 all-gather.12
  134.0 39.6 all-gather.14
  175.4 39.6 all-gather.16
  216.7 39.6 all-gather.18
  258.3 39.6 all-gather.20
  299.8 39.6 all-gather.22

commit v6 on v1

--- a/solution.py
+++ b/solution.py
@@ -38,7 +38,7 @@
     for chunk in range(width // LANES):
         lanes = pl.ds(chunk * LANES, LANES)
         for e in range(per_energy):
-            def body(t, acc, e=e, lanes=lanes):
+            def term(t, acc, e=e, lanes=lanes):
                 w = lists_ref[e * total + t]
                 u = base + e - w
                 out = list(acc)
@@ -51,10 +51,15 @@
                     out[2 * kind + 1] = out[2 * kind + 1] + (gr * wr - gi * wi)
                 return tuple(out)
 
-            zero = jnp.zeros((rows, LANES), jnp.float32)
-            acc = lax.fori_loop(0, head_ref[e], body, (zero,) * 4)
+            def pair(i, accs):
+                return term(2 * i, accs[0]), term(2 * i + 1, accs[1])
+
+            count = head_ref[e]
+            zero = (jnp.zeros((rows, LANES), jnp.float32),) * 4
+            first, second = lax.fori_loop(0, count // 2, pair, (zero, zero))
+            first = lax.fori_loop(2 * (count // 2), count, term, first)
             for comp in range(4):
-                o_ref[comp, e, :, lanes] = acc[comp] * SCALE
+                o_ref[comp, e, :, lanes] = (first[comp] + second[comp]) * SCALE
 
 
 def convolve(head, lists, whole, every, per_energy):

time: 202 us -> 192 us (0.950)
  the two profiles are of different devices: /device:TPU:193 before, /device:TPU:224 now
where the time goes in v6:
time: 192 us; the launch traced here: 188 us
  waiting for transfers between devices  123 us (64%)
  Pallas kernels  21.6 us (11%)
  blocking collectives  21.2 us (11%)
  between operations  13.5 us (7%)
  local copies, waits for them, and re-layouts  6.45 us (3%)
    all_gather x1, waiting for transfers between devices, per_device(): every = lax.all_gather(owned, 'energy', axis=1, tiled=True)  76.1 us
    all_gather x1, waiting for transfers between devices, per_device(): whole = lax.all_gather(green, 'energy', axis=1, tiled=True)  46.6 us
    pallas_call x1, Pallas kernels, convolve(): pl.pallas_call(functools.partial(conv_kernel, per_energy, total), out_sha...  21.6 us
    all_to_all x1, blocking collectives, per_device(): lax.all_to_all(outgoing, 'cell', split_axis=3, concat_axis=3, tiled=True)  21.2 us
  transfers between devices with their start and end apart: 2, of which 2 were waited for; matrix products, arithmetic and copies ran while one was open for 4% of the time, Pallas kernels for 0%

profile of v6, /device:TPU:224, one launch (start us, length us, event | category | flops | bytes accessed | tf_op | source)
XLA Modules:
  0.0 187.9 jit_solution(15874854233685097756)
XLA Ops:
  6.5 0.0 copy-start
  6.5 0.0 all-gather.4.cloned.1.call-start
  6.5 0.7 all-gather.4.cloned.1.call-update
  7.3 0.0 all-gather.6.cloned.1.call-start
  7.3 0.7 reshape.183
  8.0 0.1 copy.21
  8.1 0.1 reshape.184
  8.2 1.8 copy.26
  10.0 1.3 gather_fusion
  11.3 1.0 broadcast_select_fusion
  12.3 21.2 %all_to_all.5 = bf16[4,6,2,16,1,512]{5,2,1,0,4,3:T(2,128)(2,1)S(1)} all-to-all(bf16[4,6,2,16,1,512]{5,2,1,0,4,3:T(2,128)(2,1)S(1)} %broadcast_select_fusion), channel_id=1, replica_groups=mesh['energy'=16,'cell'=16] {'cell'}, dimensions={3} | all-to-all | bytes 1572864 | tf_op jit(solution)/shard_map/all_to_all | solution.py:95
  33.4 1.3 copy.23
  34.8 0.0 all-gather.6.cloned.1.call-update
  34.8 0.7 dynamic-slice_bitcast_fusion
  35.5 0.1 iota_compare_fusion.1
  35.6 0.1 lt.47
  35.7 0.0 copy-done
  35.7 0.1 copy.19
  35.8 0.1 squeeze.3
  35.9 0.1 iota.28
  35.9 0.1 iota.29
  36.1 0.1 fusion.2
  36.1 0.2 reduce_window_sum.11
  36.3 0.2 select_reduce_fusion
  36.5 0.1 reshape.182.lists_ref
  36.6 0.1 convert_reduce_fusion
  36.7 0.1 pad_add_fusion.head_ref
  36.8 46.6 %all-gather.4.cloned.1.call-done.g_ref = bf16[4,96,2,16,512]{4,3,2,1,0:T(8,128)(2,1)} async-done(((bf16[4,6,2,16,512]{4,3,2,1,0:T(8,128)(2,1)}), bf16[4,96,2,16,512]{4,3,2,1,0:T(8,128)(2,1)}) %all-gather.4.cloned.1.call-update) | async-done | bytes 12582928 | tf_op jit(solution)/shard_map/all_gather | solution.py:97
  83.4 76.1 %all-gather.6.cloned.1.call-done = bf16[4,96,2,16,1,512]{5,3,2,1,0,4:T(8,128)(2,1)} async-done(((bf16[4,6,2,16,1,512]{5,3,2,1,0,4:T(8,128)(2,1)}), bf16[4,96,2,16,1,512]{5,3,2,1,0,4:T(8,128)(2,1)}) %all-gather.6.cloned.1.call-update) | async-done | bytes 12582928 | tf_op jit(solution)/shard_map/all_gather | solution.py:98
  159.5 21.6 %shard_map.55 = f32[4,6,2,16,512]{4,3,2,1,0:T(8,128)} custom-call(s32[7]{0:T(128)S(1)} %pad_add_fusion.head_ref, s32[288]{0:T(512)S(1)} %reshape.182.lists_ref, bf16[4,96,2,16,512]{4,3,2,1,0:T(8,128)(2,1)} %all-gather.4.cloned.1.call-done.g_ref, bf16[4,96,2,16,512]{4,3,2,1,0:T(8,128)(2,1)} %bitcast.14), custom_call_target="tpu_custom_call" | custom-call | tf_op jit(solution)/shard_map/pallas_call | solution.py:74
  (8 shorter events, 0.1 us)
Async XLA Ops:
  6.5 29.1 %copy-start = (s32[16,16,3]{1,0,2:T(8,128)S(1)}, s32[16,16,3]{1,0,2:T(8,128)}, u32[]{:S(2)}) copy-start(s32[16,16,3]{1,0,2:T(8,128)} %param.8) | copy-start | bytes 9220
  6.5 76.8 %all-gather.4.cloned.1.call-start = ((), (), s32[]{:S(2)}) async-start(), calls=%async_computation.1 | async-start | bytes 13369344 | tf_op jit(solution)/shard_map/all_gather | solution.py:97
  7.3 152.2 %all-gather.6.cloned.1.call-start = ((), (), s32[]{:S(2)}) async-start(), calls=%async_computation.2 | async-start | bytes 13369344 | tf_op jit(solution)/shard_map/all_gather | solution.py:98
Sparse Core Ops, SparseCore 0:
  9.2 74.1 all-gather.3
  85.2 74.1 all-gather.5

commit v7 on v0

v7 whole, which is shorter than its diff:
```python
import functools

import jax
import jax.numpy as jnp
from jax import lax
from jax.experimental import pallas as pl
from jax.experimental.pallas import tpu as pltpu
from jax.sharding import PartitionSpec as P

SCALE = 0.2
LANES = 128


def multiplicity(shift_table, shift_count, group, per_energy):
    groups, slot_count = shift_table.shape[1], shift_table.shape[2]
    table_row = shift_table[group]
    counts = shift_count[group]
    slot = lax.broadcasted_iota(jnp.int32, (groups, slot_count, 1), 1)
    offset = lax.broadcasted_iota(jnp.int32, (1, 1, per_energy), 2)
    hit = (slot < counts[:, None, None]) & (table_row[:, :, None] == offset)
    return jnp.sum(hit.astype(jnp.float32), axis=1).reshape(groups * per_energy)


def ring_conv_kernel(chips, mult_ref, w_hbm, g_hbm, o_ref, g_vmem, slots,
                     g_sem, local_sem, ring_send, ring_recv, pass_send, pass_recv):
    comps, per_energy, positions, rows, width = o_ref.shape
    me = lax.axis_index("energy")
    cell = lax.axis_index("cell")
    chip, core = me // 2, me % 2
    step_dir = 1 - 2 * core
    partner = me + step_dir
    ahead = 2 * ((chip + step_dir + chips) % chips) + core
    base = me * per_energy

    def origin(k):
        return 2 * ((chip - step_dir * k + chips) % chips) + core

    def handed_slot(k):
        return 2 * ((chip + step_dir * k + chips) % chips) + 1 - core

    def remote(src, slot, send, recv, k, target):
        return pltpu.make_async_remote_copy(
            src_ref=src, dst_ref=slots.at[slot],
            send_sem=send.at[k], recv_sem=recv.at[k],
            device_id=(target, cell), device_id_type=pl.DeviceIdType.MESH,
        )

    def ring_copy(k):
        slot = origin(k - 1)
        src = w_hbm if k == 1 else slots.at[slot]
        return remote(src, slot, ring_send, ring_recv, k, ahead)

    def pass_copy(k):
        slot = origin(k)
        src = w_hbm if k == 0 else slots.at[slot]
        return remote(src, slot, pass_send, pass_recv, k, partner)

    def arrival(k):
        slot = origin(k)
        return remote(slots.at[slot], slot, ring_send, ring_recv, k, ahead)

    def handed(k):
        slot = handed_slot(k)
        return remote(slots.at[slot], slot, pass_send, pass_recv, k, partner)

    def compute(source):
        @pl.when(source <= me)
        def _():
            def over_offset(j, carry):
                weight = mult_ref[source * per_energy + j]
                lag = base - source * per_energy - j
                for p in range(positions):
                    for chunk in range(width // LANES):
                        lanes = pl.ds(chunk * LANES, LANES)
                        wv = [slots[source, comp, j, p, :, lanes].astype(jnp.float32) * weight
                              for comp in range(comps)]

                        def over_energy(e, c2, p=p, lanes=lanes, wv=wv):
                            u = lag + e

                            @pl.when(u >= 0)
                            def _():
                                for kind in range(2):
                                    gr = g_vmem[2 * kind, u, p, :, lanes].astype(jnp.float32)
                                    gi = g_vmem[2 * kind + 1, u, p, :, lanes].astype(jnp.float32)
                                    wr, wi = wv[2 * kind], wv[2 * kind + 1]
                                    o_ref[2 * kind, e, p, :, lanes] -= gr * wi + gi * wr
                                    o_ref[2 * kind + 1, e, p, :, lanes] += gr * wr - gi * wi

                            return c2

                        lax.fori_loop(0, per_energy, over_energy, 0)
                return carry

            lax.fori_loop(0, per_energy, over_offset, 0)

    g_copy = pltpu.make_async_copy(g_hbm, g_vmem, g_sem)
    g_copy.start()
    local = pltpu.make_async_copy(w_hbm, slots.at[me], local_sem)
    local.start()
    sends = [ring_copy(1), pass_copy(0)]
    for copy in sends:
        copy.start()
    o_ref[...] = jnp.zeros(o_ref.shape, o_ref.dtype)
    g_copy.wait()
    local.wait()
    compute(me)
    for k in range(1, chips):
        arrival(k).wait_recv()
        onward = [pass_copy(k)]
        if k + 1 < chips:
            onward.append(ring_copy(k + 1))
        for copy in onward:
            copy.start()
        sends.extend(onward)
        compute(origin(k))
        handed(k - 1).wait_recv()
        compute(handed_slot(k - 1))
    handed(chips - 1).wait_recv()
    compute(handed_slot(chips - 1))
    for copy in sends:
        copy.wait_send()
    o_ref[...] = o_ref[...] * SCALE


def ring_convolve(mult, owned, whole):
    groups = lax.axis_size("energy")
    chips = groups // 2
    return pl.pallas_call(
        functools.partial(ring_conv_kernel, chips),
        out_shape=jax.ShapeDtypeStruct(owned.shape, jnp.float32),
        in_specs=[
            pl.BlockSpec(memory_space=pltpu.SMEM),
            pl.BlockSpec(memory_space=pl.ANY),
            pl.BlockSpec(memory_space=pl.ANY),
        ],
        out_specs=pl.BlockSpec(memory_space=pltpu.VMEM),
        scratch_shapes=[
            pltpu.VMEM(whole.shape, whole.dtype),
            pltpu.VMEM((groups,) + owned.shape, owned.dtype),
            pltpu.SemaphoreType.DMA(()),
            pltpu.SemaphoreType.DMA(()),
            pltpu.SemaphoreType.DMA((chips,)),
            pltpu.SemaphoreType.DMA((chips,)),
            pltpu.SemaphoreType.DMA((chips,)),
            pltpu.SemaphoreType.DMA((chips,)),
        ],
        compiler_params=pltpu.CompilerParams(
            has_side_effects=True, vmem_limit_bytes=48 * 1024 * 1024
        ),
    )(mult, owned, whole)


def per_device(green, screened, cell_map, shift_table, shift_count):
    cell_count = lax.axis_size("cell")
    per_energy = green.shape[1]
    per_cell = green.shape[2]
    width = green.shape[4]
    wanted = jnp.transpose(cell_map.reshape(cell_count, per_cell)).reshape(-1)
    outgoing = jnp.take(screened, wanted, axis=2)
    outgoing = outgoing.reshape(4, per_energy, per_cell, cell_count, screened.shape[3], width)
    arrived = lax.all_to_all(outgoing, "cell", split_axis=3, concat_axis=3, tiled=True)
    owned = arrived.reshape(4, per_energy, per_cell, green.shape[3], width)
    whole = lax.all_gather(green, "energy", axis=1, tiled=True)
    group = lax.axis_index("energy")
    mult = multiplicity(shift_table, shift_count, group, per_energy)
    return ring_convolve(mult, owned, whole)


def solution(mesh):
    placed = (
        P(None, "energy", "cell", None, None),
        P(None, "energy", None, "cell", None),
        P(),
        P(),
        P(),
    )
    return jax.shard_map(
        per_device,
        mesh=mesh,
        in_specs=placed,
        out_specs=P(None, "energy", "cell", None, None),
        check_vma=False,
    )
```

time: 413 us -> 195 us (0.47)
  the two profiles are of different devices: /device:TPU:1 before, /device:TPU:224 now
where the time goes in v7:
time: 195 us
  Pallas kernels  104 us (53%)
  waiting for transfers between devices  62.6 us (32%)
  between operations  13.5 us (7%)
  starting transfers between devices  7.04 us (4%)
  local copies, waits for them, and re-layouts  6.39 us (3%)
    pallas_call x1, Pallas kernels, ring_convolve(): pl.pallas_call(functools.partial(ring_conv_kernel, chips), out_shape=jax....  104 us
    all_gather x1, waiting for transfers between devices, per_device(): whole = lax.all_gather(green, 'energy', axis=1, tiled=True)  48.3 us
    all_to_all x1, waiting for transfers between devices, per_device(): lax.all_to_all(outgoing, 'cell', split_axis=3, concat_axis=3, tiled=True)  13.6 us
    all_to_all x1, starting transfers between devices, per_device(): lax.all_to_all(outgoing, 'cell', split_axis=3, concat_axis=3, tiled=True)  7.03 us
  transfers between devices with their start and end apart: 2, of which 2 were waited for; matrix products, arithmetic and copies ran while one was open for 4% of the time, Pallas kernels for 0%

profile of v7, /device:TPU:224, one launch (start us, length us, event | category | flops | bytes accessed | tf_op | source)
XLA Modules:
  0.0 195.1 jit_solution(623297504423174980)
XLA Ops:
  6.5 0.0 copy-start
  6.5 0.0 all-gather.2.cloned.1.call-start
  6.5 0.7 all-gather.2.cloned.1.call-update
  7.3 0.7 reshape.87
  8.0 0.1 copy.21
  8.1 0.1 reshape.88
  8.2 1.8 copy.30
  9.9 1.3 gather_fusion
  11.2 1.9 broadcast_select_fusion
  13.1 7.0 %all-to-all-start = ((bf16[4,6,2,16,1,512]{5,2,1,0,4,3:T(2,128)(2,1)}), bf16[4,6,2,16,1,512]{5,2,1,0,4,3:T(2,128)(2,1)S(1)}, u32[]{:S(2)}, u32[]{:S(2)}) async-start(bf16[4,6,2,16,1,512]{5,2,1,0,4,3:T(2,128)(2,1)} %broadcast_select_fusion), calls=%async_computation | async-start | bytes 1572864 | tf_op jit(solution)/shard_map/all_to_all | solution.py:162
  20.1 0.0 copy-done
  20.2 0.7 dynamic-slice_bitcast_fusion
  20.9 0.1 copy.19
  21.0 0.1 reshape.86.mult_ref
  21.1 13.6 %all-to-all-done = bf16[4,6,2,16,1,512]{5,2,1,0,4,3:T(2,128)(2,1)S(1)} async-done(((bf16[4,6,2,16,1,512]{5,2,1,0,4,3:T(2,128)(2,1)}), bf16[4,6,2,16,1,512]{5,2,1,0,4,3:T(2,128)(2,1)S(1)}, u32[]{:S(2)}, u32[]{:S(2)}) %all-to-all-start) | async-done | bytes 786464 | tf_op jit(solution)/shard_map/all_to_all | solution.py:162
  34.6 0.4 copy.29
  35.1 48.3 %all-gather.2.cloned.1.call-done.g_hbm = bf16[4,96,2,16,512]{4,3,2,1,0:T(8,128)(2,1)} async-done(((bf16[4,6,2,16,512]{4,3,2,1,0:T(8,128)(2,1)}), bf16[4,96,2,16,512]{4,3,2,1,0:T(8,128)(2,1)}) %all-gather.2.cloned.1.call-update) | async-done | bytes 12582928 | tf_op jit(solution)/shard_map/all_gather | solution.py:164
  83.4 103.7 %shard_map.55 = f32[4,6,2,16,512]{4,3,2,1,0:T(8,128)S(1)} custom-call(f32[96]{0:T(128)S(1)} %reshape.86.mult_ref, bf16[4,6,2,16,512]{4,3,2,1,0:T(8,128)(2,1)S(1)} %bitcast.18, bf16[4,96,2,16,512]{4,3,2,1,0:T(8,128)(2,1)} %all-gather.2.cloned.1.call-done.g_hbm), custom_call_target="tpu_custom_call" | custom-call | tf_op jit(solution)/shard_map/pallas_call | solution.py:129
  187.1 1.1 copy.33
  (7 shorter events, 0.1 us)
Async XLA Ops:
  6.5 13.6 %copy-start = (s32[16,16,3]{1,0,2:T(8,128)S(1)}, s32[16,16,3]{1,0,2:T(8,128)}, u32[]{:S(2)}) copy-start(s32[16,16,3]{1,0,2:T(8,128)} %param.8) | copy-start | bytes 9220
  6.5 76.9 %all-gather.2.cloned.1.call-start = ((), (), s32[]{:S(2)}) async-start(), calls=%async_computation.1 | async-start | bytes 13369344 | tf_op jit(solution)/shard_map/all_gather | solution.py:164
  13.1 21.5 %all-to-all-start = ((bf16[4,6,2,16,1,512]{5,2,1,0,4,3:T(2,128)(2,1)}), bf16[4,6,2,16,1,512]{5,2,1,0,4,3:T(2,128)(2,1)S(1)}, u32[]{:S(2)}, u32[]{:S(2)}) async-start(bf16[4,6,2,16,1,512]{5,2,1,0,4,3:T(2,128)(2,1)} %broadcast_select_fusion), calls=%async_computation | async-start | bytes 1572864 | tf_op jit(solution)/shard_map/all_to_all | solution.py:162
Sparse Core Ops, SparseCore 0:
  9.2 74.1 all-gather.1

commit v8 on v7

v8 whole, which is shorter than its diff:
```python
import functools

import jax
import jax.numpy as jnp
from jax import lax
from jax.experimental import pallas as pl
from jax.experimental.pallas import tpu as pltpu
from jax.sharding import PartitionSpec as P

SCALE = 0.2
LANES = 128


def slot_tables(shift_table, shift_count, group):
    groups, slot_count = shift_table.shape[1], shift_table.shape[2]
    slot = lax.broadcasted_iota(jnp.int32, (groups, slot_count), 1)
    live = (slot < shift_count[group][:, None]).astype(jnp.float32)
    return shift_table[group].reshape(-1), live.reshape(-1)


def ring_conv_kernel(chips, slot_count, shift_ref, live_ref, w_hbm, g_hbm, o_ref, g_vmem, *scratch):
    own_buf = scratch[0]
    ring_bufs = (None,) + tuple(scratch[1:chips])
    hand_bufs = tuple(scratch[chips:2 * chips])
    g_sem, local_sem, ring_send, ring_recv, pass_send, pass_recv = scratch[2 * chips:]
    comps, per_energy, positions, rows, width = o_ref.shape
    me = lax.axis_index("energy")
    cell = lax.axis_index("cell")
    chip, core = me // 2, me % 2
    step_dir = 1 - 2 * core
    partner = me + step_dir
    ahead = 2 * ((chip + step_dir + chips) % chips) + core
    base = me * per_energy

    def origin(k):
        return 2 * ((chip - step_dir * k + chips) % chips) + core

    def handed_group(k):
        return 2 * ((chip + step_dir * k + chips) % chips) + 1 - core

    def remote(src, dst, send, recv, k, target):
        return pltpu.make_async_remote_copy(
            src_ref=src, dst_ref=dst, send_sem=send.at[k], recv_sem=recv.at[k],
            device_id=(target, cell), device_id_type=pl.DeviceIdType.MESH,
        )

    def ring_copy(k):
        src = w_hbm if k == 1 else ring_bufs[k - 1]
        return remote(src, ring_bufs[k], ring_send, ring_recv, k, ahead)

    def pass_copy(k):
        src = w_hbm if k == 0 else ring_bufs[k]
        return remote(src, hand_bufs[k], pass_send, pass_recv, k, partner)

    def arrival(k):
        return remote(ring_bufs[k], ring_bufs[k], ring_send, ring_recv, k, ahead)

    def handed(k):
        return remote(hand_bufs[k], hand_bufs[k], pass_send, pass_recv, k, partner)

    def compute(source, buf, masked):
        lag = base - source * per_energy

        def run():
            for p in range(positions):
                for chunk in range(width // LANES):
                    lanes = pl.ds(chunk * LANES, LANES)

                    def over_energy(e, carry, p=p, lanes=lanes):
                        acc = [jnp.zeros((rows, LANES), jnp.float32)] * comps
                        for c in range(slot_count):
                            j = shift_ref[source * slot_count + c]
                            weight = live_ref[source * slot_count + c]
                            u = lag + e - j
                            if masked:
                                weight = jnp.where(u >= 0, weight, 0.0)
                                u = jnp.maximum(u, 0)
                            for kind in range(2):
                                gr = g_vmem[2 * kind, u, p, :, lanes].astype(jnp.float32)
                                gi = g_vmem[2 * kind + 1, u, p, :, lanes].astype(jnp.float32)
                                wr = buf[2 * kind, j, p, :, lanes].astype(jnp.float32) * weight
                                wi = buf[2 * kind + 1, j, p, :, lanes].astype(jnp.float32) * weight
                                acc[2 * kind] = acc[2 * kind] - (gr * wi + gi * wr)
                                acc[2 * kind + 1] = acc[2 * kind + 1] + (gr * wr - gi * wi)
                        for comp in range(comps):
                            o_ref[comp, e, p, :, lanes] += acc[comp]
                        return carry

                    lax.fori_loop(0, per_energy, over_energy, 0)

        if masked:
            run()
        else:
            pl.when(source < me)(run)

    g_copy = pltpu.make_async_copy(g_hbm, g_vmem, g_sem)
    g_copy.start()
    local = pltpu.make_async_copy(w_hbm, own_buf, local_sem)
    local.start()
    sends = [ring_copy(1), pass_copy(0)]
    for copy in sends:
        copy.start()
    o_ref[...] = jnp.zeros(o_ref.shape, o_ref.dtype)
    g_copy.wait()
    local.wait()
    compute(me, own_buf, True)
    for k in range(1, chips):
        arrival(k).wait_recv()
        onward = [pass_copy(k)]
        if k + 1 < chips:
            onward.append(ring_copy(k + 1))
        for copy in onward:
            copy.start()
        sends.extend(onward)
        compute(origin(k), ring_bufs[k], False)
        handed(k - 1).wait_recv()
        compute(handed_group(k - 1), hand_bufs[k - 1], False)
    handed(chips - 1).wait_recv()
    compute(handed_group(chips - 1), hand_bufs[chips - 1], False)
    for copy in sends:
        copy.wait_send()
    o_ref[...] = o_ref[...] * SCALE


def ring_convolve(shifts, lives, owned, whole, slot_count):
    groups = lax.axis_size("energy")
    chips = groups // 2
    block = pltpu.VMEM(owned.shape, owned.dtype)
    return pl.pallas_call(
        functools.partial(ring_conv_kernel, chips, slot_count),
        out_shape=jax.ShapeDtypeStruct(owned.shape, jnp.float32),
        in_specs=[
            pl.BlockSpec(memory_space=pltpu.SMEM),
            pl.BlockSpec(memory_space=pltpu.SMEM),
            pl.BlockSpec(memory_space=pl.ANY),
            pl.BlockSpec(memory_space=pl.ANY),
        ],
        out_specs=pl.BlockSpec(memory_space=pltpu.VMEM),
        scratch_shapes=[pltpu.VMEM(whole.shape, whole.dtype)]
        + [block] * (2 * chips)
        + [
            pltpu.SemaphoreType.DMA(()),
            pltpu.SemaphoreType.DMA(()),
            pltpu.SemaphoreType.DMA((chips,)),
            pltpu.SemaphoreType.DMA((chips,)),
            pltpu.SemaphoreType.DMA((chips,)),
            pltpu.SemaphoreType.DMA((chips,)),
        ],
        compiler_params=pltpu.CompilerParams(
            has_side_effects=True, vmem_limit_bytes=48 * 1024 * 1024
        ),
    )(shifts, lives, owned, whole)


def per_device(green, screened, cell_map, shift_table, shift_count):
    cell_count = lax.axis_size("cell")
    per_energy = green.shape[1]
    per_cell = green.shape[2]
    width = green.shape[4]
    wanted = jnp.transpose(cell_map.reshape(cell_count, per_cell)).reshape(-1)
    outgoing = jnp.take(screened, wanted, axis=2)
    outgoing = outgoing.reshape(4, per_energy, per_cell, cell_count, screened.shape[3], width)
    arrived = lax.all_to_all(outgoing, "cell", split_axis=3, concat_axis=3, tiled=True)
    owned = arrived.reshape(4, per_energy, per_cell, green.shape[3], width)
    whole = lax.all_gather(green, "energy", axis=1, tiled=True)
    group = lax.axis_index("energy")
    shifts, lives = slot_tables(shift_table, shift_count, group)
    return ring_convolve(shifts, lives, owned, whole, shift_table.shape[2])


def solution(mesh):
    placed = (
        P(None, "energy", "cell", None, None),
        P(None, "energy", None, "cell", None),
        P(),
        P(),
        P(),
    )
    return jax.shard_map(
        per_device,
        mesh=mesh,
        in_specs=placed,
        out_specs=P(None, "energy", "cell", None, None),
        check_vma=False,
    )
```

time: 195 us -> 188 us (0.964); the launches traced: 195 us -> 185 us
  Pallas kernels: 104 us -> 93.3 us
    pallas_call x1, Pallas kernels: 104 us -> 93.3 us  [ring_convolve(): pl.pallas_call(functools.partial(ring_conv_kernel, chips, slot_count), ou...]
where the time goes in v8:
time: 188 us; the launch traced here: 185 us
  Pallas kernels  93.3 us (50%)
  waiting for transfers between devices  62.4 us (33%)
  between operations  13.5 us (7%)
  starting transfers between devices  7.04 us (4%)
  local copies, waits for them, and re-layouts  6.49 us (3%)
  other arithmetic  1.95 us (1%)
    pallas_call x1, Pallas kernels, ring_convolve(): pl.pallas_call(functools.partial(ring_conv_kernel, chips, slot_count), ou...  93.3 us
    all_gather x1, waiting for transfers between devices, per_device(): whole = lax.all_gather(green, 'energy', axis=1, tiled=True)  48.3 us
    all_to_all x1, waiting for transfers between devices, per_device(): lax.all_to_all(outgoing, 'cell', split_axis=3, concat_axis=3, tiled=True)  13.4 us
    all_to_all x1, starting transfers between devices, per_device(): lax.all_to_all(outgoing, 'cell', split_axis=3, concat_axis=3, tiled=True)  7.03 us
  transfers between devices with their start and end apart: 2, of which 2 were waited for; matrix products, arithmetic and copies ran while one was open for 4% of the time, Pallas kernels for 0%

profile of v8, /device:TPU:224, one launch (start us, length us, event | category | flops | bytes accessed | tf_op | source)
XLA Modules:
  0.0 184.6 jit_solution(8208270599394188262)
XLA Ops:
  6.5 0.0 copy-start
  6.5 0.0 all-gather.2.cloned.1.call-start
  6.5 0.7 all-gather.2.cloned.1.call-update
  7.3 0.7 reshape.64
  8.0 0.1 copy.16
  8.1 0.1 reshape.65
  8.2 1.8 copy.23
  9.9 1.3 gather_fusion
  11.2 1.9 %broadcast_select_fusion = bf16[4,6,2,16,1,512]{5,2,1,0,4,3:T(2,128)(2,1)} fusion(pred[2,16]{0,1:T(8,128)(4,1)S(1)} %compare_and_fusion, bf16[4,6,2,16,1,512]{5,0,1,3,2,4:T(4,128)(2,1)S(1)} %bitcast.17), kind=kLoop, calls=%fused_computation.1 | loop fusion | flops 393216 | bytes 1572896 | tf_op jit(solution)/shard_map/jit(_take)/select_n | solution.py:161
  13.1 7.0 %all-to-all-start = ((bf16[4,6,2,16,1,512]{5,2,1,0,4,3:T(2,128)(2,1)}), bf16[4,6,2,16,1,512]{5,2,1,0,4,3:T(2,128)(2,1)S(1)}, u32[]{:S(2)}, u32[]{:S(2)}) async-start(bf16[4,6,2,16,1,512]{5,2,1,0,4,3:T(2,128)(2,1)} %broadcast_select_fusion), calls=%async_computation | async-start | bytes 1572864 | tf_op jit(solution)/shard_map/all_to_all | solution.py:163
  20.1 0.0 copy-done
  20.2 0.1 copy.14
  20.3 0.1 reshape_squeeze.3.shift_ref
  20.3 0.7 dynamic-slice_bitcast_fusion
  21.1 0.1 fusion
  21.1 0.1 reshape.67.live_ref
  21.2 13.4 %all-to-all-done = bf16[4,6,2,16,1,512]{5,2,1,0,4,3:T(2,128)(2,1)S(1)} async-done(((bf16[4,6,2,16,1,512]{5,2,1,0,4,3:T(2,128)(2,1)}), bf16[4,6,2,16,1,512]{5,2,1,0,4,3:T(2,128)(2,1)S(1)}, u32[]{:S(2)}, u32[]{:S(2)}) %all-to-all-start) | async-done | bytes 786464 | tf_op jit(solution)/shard_map/all_to_all | solution.py:163
  34.6 0.4 copy.22
  35.1 48.3 %all-gather.2.cloned.1.call-done.g_hbm = bf16[4,96,2,16,512]{4,3,2,1,0:T(8,128)(2,1)} async-done(((bf16[4,6,2,16,512]{4,3,2,1,0:T(8,128)(2,1)}), bf16[4,96,2,16,512]{4,3,2,1,0:T(8,128)(2,1)}) %all-gather.2.cloned.1.call-update) | async-done | bytes 12582928 | tf_op jit(solution)/shard_map/all_gather | solution.py:165
  83.4 93.3 %shard_map.55 = f32[4,6,2,16,512]{4,3,2,1,0:T(8,128)S(1)} custom-call(s32[48]{0:T(128)S(1)} %reshape_squeeze.3.shift_ref, f32[48]{0:T(128)S(1)} %reshape.67.live_ref, bf16[4,6,2,16,512]{4,3,2,1,0:T(8,128)(2,1)S(1)} %bitcast.15, bf16[4,96,2,16,512]{4,3,2,1,0:T(8,128)(2,1)} %all-gather.2.cloned.1.call-done.g_hbm), custom_call_target="tpu_custom_call" | custom-call | tf_op jit(solution)/shard_map/pallas_call | solution.py:129
  176.6 1.1 copy.25
  (4 shorter events, 0.0 us)
Async XLA Ops:
  6.5 13.6 %copy-start = (s32[16,16,3]{1,0,2:T(8,128)S(1)}, s32[16,16,3]{1,0,2:T(8,128)}, u32[]{:S(2)}) copy-start(s32[16,16,3]{1,0,2:T(8,128)} %param.8) | copy-start | bytes 9220
  6.5 76.8 %all-gather.2.cloned.1.call-start = ((), (), s32[]{:S(2)}) async-start(), calls=%async_computation.1 | async-start | bytes 13369344 | tf_op jit(solution)/shard_map/all_gather | solution.py:165
  13.1 21.5 %all-to-all-start = ((bf16[4,6,2,16,1,512]{5,2,1,0,4,3:T(2,128)(2,1)}), bf16[4,6,2,16,1,512]{5,2,1,0,4,3:T(2,128)(2,1)S(1)}, u32[]{:S(2)}, u32[]{:S(2)}) async-start(bf16[4,6,2,16,1,512]{5,2,1,0,4,3:T(2,128)(2,1)} %broadcast_select_fusion), calls=%async_computation | async-start | bytes 1572864 | tf_op jit(solution)/shard_map/all_to_all | solution.py:163
Sparse Core Ops, SparseCore 0:
  9.2 74.1 all-gather.1

commit v9 on v8

v9 whole, which is shorter than its diff:
```python
import functools

import jax
import jax.numpy as jnp
from jax import lax
from jax.experimental import pallas as pl
from jax.experimental.pallas import tpu as pltpu
from jax.sharding import PartitionSpec as P

SCALE = 0.2
LANES = 128


def slot_tables(shift_table, shift_count, group):
    groups, slot_count = shift_table.shape[1], shift_table.shape[2]
    slot = lax.broadcasted_iota(jnp.int32, (groups, slot_count), 1)
    live = (slot < shift_count[group][:, None]).astype(jnp.float32)
    return shift_table[group].reshape(-1), live.reshape(-1)


def ring_conv_kernel(chips, slot_count, shift_ref, live_ref, w_hbm, g_hbm, o_ref, g_vmem, *scratch):
    halves = 2
    count = 2 * chips
    bufs = [scratch[h * count:(h + 1) * count] for h in range(halves)]
    own_bufs = [b[0] for b in bufs]
    ring_bufs = [(None,) + tuple(b[1:chips]) for b in bufs]
    hand_bufs = [tuple(b[chips:count]) for b in bufs]
    g_sem, local_sem, ring_send, ring_recv, pass_send, pass_recv = scratch[halves * count:]
    comps, per_energy, positions, rows, width = o_ref.shape
    me = lax.axis_index("energy")
    cell = lax.axis_index("cell")
    chip, core = me // 2, me % 2
    step_dir = 1 - 2 * core
    partner = me + step_dir
    ahead = 2 * ((chip + step_dir + chips) % chips) + core
    base = me * per_energy

    def origin(k):
        return 2 * ((chip - step_dir * k + chips) % chips) + core

    def handed_group(k):
        return 2 * ((chip + step_dir * k + chips) % chips) + 1 - core

    def own_half(h):
        return w_hbm.at[pl.ds(2 * h, 2)]

    def remote(src, dst, send, recv, k, h, target):
        return pltpu.make_async_remote_copy(
            src_ref=src, dst_ref=dst, send_sem=send.at[k, h], recv_sem=recv.at[k, h],
            device_id=(target, cell), device_id_type=pl.DeviceIdType.MESH,
        )

    def ring_copy(k, h):
        src = own_half(h) if k == 1 else ring_bufs[h][k - 1]
        return remote(src, ring_bufs[h][k], ring_send, ring_recv, k, h, ahead)

    def pass_copy(k, h):
        src = own_half(h) if k == 0 else ring_bufs[h][k]
        return remote(src, hand_bufs[h][k], pass_send, pass_recv, k, h, partner)

    def arrival(k, h):
        return remote(ring_bufs[h][k], ring_bufs[h][k], ring_send, ring_recv, k, h, ahead)

    def handed(k, h):
        return remote(hand_bufs[h][k], hand_bufs[h][k], pass_send, pass_recv, k, h, partner)

    def compute(source, buf, kind, masked):
        lag = base - source * per_energy

        def run():
            for p in range(positions):
                for chunk in range(width // LANES):
                    lanes = pl.ds(chunk * LANES, LANES)

                    def over_energy(e, carry, p=p, lanes=lanes):
                        real = jnp.zeros((rows, LANES), jnp.float32)
                        imag = jnp.zeros((rows, LANES), jnp.float32)
                        for c in range(slot_count):
                            j = shift_ref[source * slot_count + c]
                            weight = live_ref[source * slot_count + c]
                            u = lag + e - j
                            if masked:
                                weight = jnp.where(u >= 0, weight, 0.0)
                                u = jnp.maximum(u, 0)
                            gr = g_vmem[2 * kind, u, p, :, lanes].astype(jnp.float32)
                            gi = g_vmem[2 * kind + 1, u, p, :, lanes].astype(jnp.float32)
                            wr = buf[0, j, p, :, lanes].astype(jnp.float32) * weight
                            wi = buf[1, j, p, :, lanes].astype(jnp.float32) * weight
                            real = real - (gr * wi + gi * wr)
                            imag = imag + (gr * wr - gi * wi)
                        o_ref[2 * kind, e, p, :, lanes] += real
                        o_ref[2 * kind + 1, e, p, :, lanes] += imag
                        return carry

                    lax.fori_loop(0, per_energy, over_energy, 0)

        if masked:
            run()
        else:
            pl.when(source < me)(run)

    g_copy = pltpu.make_async_copy(g_hbm, g_vmem, g_sem)
    g_copy.start()
    locals_ = [pltpu.make_async_copy(own_half(h), own_bufs[h], local_sem.at[h]) for h in range(halves)]
    for copy in locals_:
        copy.start()
    sends = [ring_copy(1, h) for h in range(halves)] + [pass_copy(0, h) for h in range(halves)]
    for copy in sends:
        copy.start()
    o_ref[...] = jnp.zeros(o_ref.shape, o_ref.dtype)
    g_copy.wait()
    for h in range(halves):
        locals_[h].wait()
        compute(me, own_bufs[h], h, True)
    for k in range(1, chips):
        for h in range(halves):
            arrival(k, h).wait_recv()
            onward = [pass_copy(k, h)]
            if k + 1 < chips:
                onward.append(ring_copy(k + 1, h))
            for copy in onward:
                copy.start()
            sends.extend(onward)
            compute(origin(k), ring_bufs[h][k], h, False)
        for h in range(halves):
            handed(k - 1, h).wait_recv()
            compute(handed_group(k - 1), hand_bufs[h][k - 1], h, False)
    for h in range(halves):
        handed(chips - 1, h).wait_recv()
        compute(handed_group(chips - 1), hand_bufs[h][chips - 1], h, False)
    for copy in sends:
        copy.wait_send()
    o_ref[...] = o_ref[...] * SCALE


def ring_convolve(shifts, lives, owned, whole, slot_count):
    groups = lax.axis_size("energy")
    chips = groups // 2
    half = pltpu.VMEM((owned.shape[0] // 2,) + owned.shape[1:], owned.dtype)
    return pl.pallas_call(
        functools.partial(ring_conv_kernel, chips, slot_count),
        out_shape=jax.ShapeDtypeStruct(owned.shape, jnp.float32),
        in_specs=[
            pl.BlockSpec(memory_space=pltpu.SMEM),
            pl.BlockSpec(memory_space=pltpu.SMEM),
            pl.BlockSpec(memory_space=pl.ANY),
            pl.BlockSpec(memory_space=pl.ANY),
        ],
        out_specs=pl.BlockSpec(memory_space=pltpu.VMEM),
        scratch_shapes=[pltpu.VMEM(whole.shape, whole.dtype)]
        + [half] * (4 * chips)
        + [
            pltpu.SemaphoreType.DMA(()),
            pltpu.SemaphoreType.DMA((2,)),
            pltpu.SemaphoreType.DMA((chips, 2)),
            pltpu.SemaphoreType.DMA((chips, 2)),
            pltpu.SemaphoreType.DMA((chips, 2)),
            pltpu.SemaphoreType.DMA((chips, 2)),
        ],
        compiler_params=pltpu.CompilerParams(
            has_side_effects=True, vmem_limit_bytes=48 * 1024 * 1024
        ),
    )(shifts, lives, owned, whole)


def per_device(green, screened, cell_map, shift_table, shift_count):
    cell_count = lax.axis_size("cell")
    per_energy = green.shape[1]
    per_cell = green.shape[2]
    width = green.shape[4]
    wanted = jnp.transpose(cell_map.reshape(cell_count, per_cell)).reshape(-1)
    outgoing = jnp.take(screened, wanted, axis=2)
    outgoing = outgoing.reshape(4, per_energy, per_cell, cell_count, screened.shape[3], width)
    arrived = lax.all_to_all(outgoing, "cell", split_axis=3, concat_axis=3, tiled=True)
    owned = arrived.reshape(4, per_energy, per_cell, green.shape[3], width)
    whole = lax.all_gather(green, "energy", axis=1, tiled=True)
    group = lax.axis_index("energy")
    shifts, lives = slot_tables(shift_table, shift_count, group)
    return ring_convolve(shifts, lives, owned, whole, shift_table.shape[2])


def solution(mesh):
    placed = (
        P(None, "energy", "cell", None, None),
        P(None, "energy", None, "cell", None),
        P(),
        P(),
        P(),
    )
    return jax.shard_map(
        per_device,
        mesh=mesh,
        in_specs=placed,
        out_specs=P(None, "energy", "cell", None, None),
        check_vma=False,
    )
```

time: 188 us -> 174 us (0.926)
  Pallas kernels: 93.3 us -> 79.8 us
    pallas_call x1, Pallas kernels: 93.3 us -> 79.8 us  [ring_convolve(): pl.pallas_call(functools.partial(ring_conv_kernel, chips, slot_count), ou...]
where the time goes in v9:
time: 174 us; the launch traced here: 171 us
  Pallas kernels  79.8 us (46%)
  waiting for transfers between devices  62.4 us (36%)
  between operations  13.5 us (8%)
  starting transfers between devices  7.04 us (4%)
  local copies, waits for them, and re-layouts  6.49 us (4%)
  other arithmetic  1.95 us (1%)
    pallas_call x1, Pallas kernels, ring_convolve(): pl.pallas_call(functools.partial(ring_conv_kernel, chips, slot_count), ou...  79.8 us
    all_gather x1, waiting for transfers between devices, per_device(): whole = lax.all_gather(green, 'energy', axis=1, tiled=True)  48.3 us
    all_to_all x1, waiting for transfers between devices, per_device(): lax.all_to_all(outgoing, 'cell', split_axis=3, concat_axis=3, tiled=True)  13.4 us
    all_to_all x1, starting transfers between devices, per_device(): lax.all_to_all(outgoing, 'cell', split_axis=3, concat_axis=3, tiled=True)  7.03 us
  transfers between devices with their start and end apart: 2, of which 2 were waited for; matrix products, arithmetic and copies ran while one was open for 4% of the time, Pallas kernels for 0%

profile of v9, /device:TPU:224, one launch (start us, length us, event | category | flops | bytes accessed | tf_op | source)
XLA Modules:
  0.0 171.2 jit_solution(1212940153886927495)
XLA Ops:
  6.5 0.0 copy-start
  6.5 0.0 all-gather.2.cloned.1.call-start
  6.5 0.7 all-gather.2.cloned.1.call-update
  7.3 0.7 reshape.64
  8.0 0.1 copy.16
  8.1 0.1 reshape.65
  8.2 1.8 %copy.23 = bf16[4,6,32,1,512]{4,0,2,1,3:T(4,128)(2,1)S(1)} copy(bf16[4,6,32,1,512]{4,2,3,1,0:T(8,128)(2,1)} %param.6) | data formatting | bytes 1572864 | tf_op args[1]
  9.9 1.3 gather_fusion
  11.2 1.9 %broadcast_select_fusion = bf16[4,6,2,16,1,512]{5,2,1,0,4,3:T(2,128)(2,1)} fusion(pred[2,16]{0,1:T(8,128)(4,1)S(1)} %compare_and_fusion, bf16[4,6,2,16,1,512]{5,0,1,3,2,4:T(4,128)(2,1)S(1)} %bitcast.17), kind=kLoop, calls=%fused_computation.1 | loop fusion | flops 393216 | bytes 1572896 | tf_op jit(solution)/shard_map/jit(_take)/select_n | solution.py:172
  13.1 7.0 %all-to-all-start = ((bf16[4,6,2,16,1,512]{5,2,1,0,4,3:T(2,128)(2,1)}), bf16[4,6,2,16,1,512]{5,2,1,0,4,3:T(2,128)(2,1)S(1)}, u32[]{:S(2)}, u32[]{:S(2)}) async-start(bf16[4,6,2,16,1,512]{5,2,1,0,4,3:T(2,128)(2,1)} %broadcast_select_fusion), calls=%async_computation | async-start | bytes 1572864 | tf_op jit(solution)/shard_map/all_to_all | solution.py:174
  20.1 0.0 copy-done
  20.2 0.1 copy.14
  20.2 0.1 reshape_squeeze.3.shift_ref
  20.3 0.7 dynamic-slice_bitcast_fusion
  21.1 0.1 fusion
  21.1 0.1 reshape.67.live_ref
  21.2 13.4 %all-to-all-done = bf16[4,6,2,16,1,512]{5,2,1,0,4,3:T(2,128)(2,1)S(1)} async-done(((bf16[4,6,2,16,1,512]{5,2,1,0,4,3:T(2,128)(2,1)}), bf16[4,6,2,16,1,512]{5,2,1,0,4,3:T(2,128)(2,1)S(1)}, u32[]{:S(2)}, u32[]{:S(2)}) %all-to-all-start) | async-done | bytes 786464 | tf_op jit(solution)/shard_map/all_to_all | solution.py:174
  34.6 0.4 copy.22
  35.1 48.3 %all-gather.2.cloned.1.call-done.g_hbm = bf16[4,96,2,16,512]{4,3,2,1,0:T(8,128)(2,1)} async-done(((bf16[4,6,2,16,512]{4,3,2,1,0:T(8,128)(2,1)}), bf16[4,96,2,16,512]{4,3,2,1,0:T(8,128)(2,1)}) %all-gather.2.cloned.1.call-update) | async-done | bytes 12582928 | tf_op jit(solution)/shard_map/all_gather | solution.py:176
  83.4 79.8 %shard_map.55 = f32[4,6,2,16,512]{4,3,2,1,0:T(8,128)S(1)} custom-call(s32[48]{0:T(128)S(1)} %reshape_squeeze.3.shift_ref, f32[48]{0:T(128)S(1)} %reshape.67.live_ref, bf16[4,6,2,16,512]{4,3,2,1,0:T(8,128)(2,1)S(1)} %bitcast.15, bf16[4,96,2,16,512]{4,3,2,1,0:T(8,128)(2,1)} %all-gather.2.cloned.1.call-done.g_hbm), custom_call_target="tpu_custom_call" | custom-call | tf_op jit(solution)/shard_map/pallas_call | solution.py:140
  163.2 1.1 copy.25
  (4 shorter events, 0.0 us)
Async XLA Ops:
  6.5 13.6 %copy-start = (s32[16,16,3]{1,0,2:T(8,128)S(1)}, s32[16,16,3]{1,0,2:T(8,128)}, u32[]{:S(2)}) copy-start(s32[16,16,3]{1,0,2:T(8,128)} %param.8) | copy-start | bytes 9220
  6.5 76.8 %all-gather.2.cloned.1.call-start = ((), (), s32[]{:S(2)}) async-start(), calls=%async_computation.1 | async-start | bytes 13369344 | tf_op jit(solution)/shard_map/all_gather | solution.py:176
  13.1 21.5 %all-to-all-start = ((bf16[4,6,2,16,1,512]{5,2,1,0,4,3:T(2,128)(2,1)}), bf16[4,6,2,16,1,512]{5,2,1,0,4,3:T(2,128)(2,1)S(1)}, u32[]{:S(2)}, u32[]{:S(2)}) async-start(bf16[4,6,2,16,1,512]{5,2,1,0,4,3:T(2,128)(2,1)} %broadcast_select_fusion), calls=%async_computation | async-start | bytes 1572864 | tf_op jit(solution)/shard_map/all_to_all | solution.py:174
Sparse Core Ops, SparseCore 0:
  9.2 74.1 all-gather.1

commit v10 on v9

--- a/solution.py
+++ b/solution.py
@@ -9,6 +9,7 @@
 
 SCALE = 0.2
 LANES = 128
+PIECE = 256
 
 
 def slot_tables(shift_table, shift_count, group):
@@ -19,7 +20,8 @@
 
 
 def ring_conv_kernel(chips, slot_count, shift_ref, live_ref, w_hbm, g_hbm, o_ref, g_vmem, *scratch):
-    halves = 2
+    lane_parts = o_ref.shape[4] // PIECE
+    halves = 2 * lane_parts
     count = 2 * chips
     bufs = [scratch[h * count:(h + 1) * count] for h in range(halves)]
     own_bufs = [b[0] for b in bufs]
@@ -42,7 +44,8 @@
         return 2 * ((chip + step_dir * k + chips) % chips) + 1 - core
 
     def own_half(h):
-        return w_hbm.at[pl.ds(2 * h, 2)]
+        kind, part = h // lane_parts, h % lane_parts
+        return w_hbm.at[pl.ds(2 * kind, 2), :, :, :, pl.ds(part * PIECE, PIECE)]
 
     def remote(src, dst, send, recv, k, h, target):
         return pltpu.make_async_remote_copy(
@@ -64,15 +67,17 @@
     def handed(k, h):
         return remote(hand_bufs[h][k], hand_bufs[h][k], pass_send, pass_recv, k, h, partner)
 
-    def compute(source, buf, kind, masked):
+    def compute(source, buf, h, masked):
         lag = base - source * per_energy
+        kind, part = h // lane_parts, h % lane_parts
 
         def run():
             for p in range(positions):
-                for chunk in range(width // LANES):
-                    lanes = pl.ds(chunk * LANES, LANES)
-
-                    def over_energy(e, carry, p=p, lanes=lanes):
+                for chunk in range(PIECE // LANES):
+                    local = pl.ds(chunk * LANES, LANES)
+                    lanes = pl.ds(part * PIECE + chunk * LANES, LANES)
+
+                    def over_energy(e, carry, p=p, lanes=lanes, local=local):
                         real = jnp.zeros((rows, LANES), jnp.float32)
                         imag = jnp.zeros((rows, LANES), jnp.float32)
                         for c in range(slot_count):
@@ -84,8 +89,8 @@
                                 u = jnp.maximum(u, 0)
                             gr = g_vmem[2 * kind, u, p, :, lanes].astype(jnp.float32)
                             gi = g_vmem[2 * kind + 1, u, p, :, lanes].astype(jnp.float32)
-                            wr = buf[0, j, p, :, lanes].astype(jnp.float32) * weight
-                            wi = buf[1, j, p, :, lanes].astype(jnp.float32) * weight
+                            wr = buf[0, j, p, :, local].astype(jnp.float32) * weight
+                            wi = buf[1, j, p, :, local].astype(jnp.float32) * weight
                             real = real - (gr * wi + gi * wr)
                             imag = imag + (gr * wr - gi * wi)
                         o_ref[2 * kind, e, p, :, lanes] += real
@@ -136,7 +141,8 @@
 def ring_convolve(shifts, lives, owned, whole, slot_count):
     groups = lax.axis_size("energy")
     chips = groups // 2
-    half = pltpu.VMEM((owned.shape[0] // 2,) + owned.shape[1:], owned.dtype)
+    pieces = 2 * (owned.shape[4] // PIECE)
+    half = pltpu.VMEM((owned.shape[0] // 2,) + owned.shape[1:4] + (PIECE,), owned.dtype)
     return pl.pallas_call(
         functools.partial(ring_conv_kernel, chips, slot_count),
         out_shape=jax.ShapeDtypeStruct(owned.shape, jnp.float32),
@@ -148,14 +154,14 @@
         ],
         out_specs=pl.BlockSpec(memory_space=pltpu.VMEM),
         scratch_shapes=[pltpu.VMEM(whole.shape, whole.dtype)]
-        + [half] * (4 * chips)
+        + [half] * (2 * chips * pieces)
         + [
             pltpu.SemaphoreType.DMA(()),
-            pltpu.SemaphoreType.DMA((2,)),
-            pltpu.SemaphoreType.DMA((chips, 2)),
-            pltpu.SemaphoreType.DMA((chips, 2)),
-            pltpu.SemaphoreType.DMA((chips, 2)),
-            pltpu.SemaphoreType.DMA((chips, 2)),
+            pltpu.SemaphoreType.DMA((pieces,)),
+            pltpu.SemaphoreType.DMA((chips, pieces)),
+            pltpu.SemaphoreType.DMA((chips, pieces)),
+            pltpu.SemaphoreType.DMA((chips, pieces)),
+            pltpu.SemaphoreType.DMA((chips, pieces)),
         ],
         compiler_params=pltpu.CompilerParams(
             has_side_effects=True, vmem_limit_bytes=48 * 1024 * 1024

time: 174 us -> 174 us (level)
  no operation moved by 1% of the time
where the time goes in v10:
time: 174 us; the launch traced here: 171 us
  Pallas kernels  79.7 us (46%)
  waiting for transfers between devices  62.4 us (36%)
  between operations  13.5 us (8%)
  starting transfers between devices  7.04 us (4%)
  local copies, waits for them, and re-layouts  6.49 us (4%)
  other arithmetic  1.95 us (1%)
    pallas_call x1, Pallas kernels, ring_convolve(): pl.pallas_call(functools.partial(ring_conv_kernel, chips, slot_count), ou...  79.7 us
    all_gather x1, waiting for transfers between devices, per_device(): whole = lax.all_gather(green, 'energy', axis=1, tiled=True)  48.3 us
    all_to_all x1, waiting for transfers between devices, per_device(): lax.all_to_all(outgoing, 'cell', split_axis=3, concat_axis=3, tiled=True)  13.4 us
    all_to_all x1, starting transfers between devices, per_device(): lax.all_to_all(outgoing, 'cell', split_axis=3, concat_axis=3, tiled=True)  7.03 us
  transfers between devices with their start and end apart: 2, of which 2 were waited for; matrix products, arithmetic and copies ran while one was open for 4% of the time, Pallas kernels for 0%

profile of v10, /device:TPU:224, one launch (start us, length us, event | category | flops | bytes accessed | tf_op | source)
XLA Modules:
  0.0 171.1 jit_solution(15313107610755571458)
XLA Ops:
  6.5 0.0 copy-start
  6.5 0.0 all-gather.2.cloned.1.call-start
  6.5 0.7 all-gather.2.cloned.1.call-update
  7.3 0.7 reshape.64
  8.0 0.1 copy.16
  8.1 0.1 reshape.65
  8.2 1.8 %copy.23 = bf16[4,6,32,1,512]{4,0,2,1,3:T(4,128)(2,1)S(1)} copy(bf16[4,6,32,1,512]{4,2,3,1,0:T(8,128)(2,1)} %param.6) | data formatting | bytes 1572864 | tf_op args[1]
  9.9 1.3 gather_fusion
  11.2 1.9 %broadcast_select_fusion = bf16[4,6,2,16,1,512]{5,2,1,0,4,3:T(2,128)(2,1)} fusion(pred[2,16]{0,1:T(8,128)(4,1)S(1)} %compare_and_fusion, bf16[4,6,2,16,1,512]{5,0,1,3,2,4:T(4,128)(2,1)S(1)} %bitcast.17), kind=kLoop, calls=%fused_computation.1 | loop fusion | flops 393216 | bytes 1572896 | tf_op jit(solution)/shard_map/jit(_take)/select_n | solution.py:178
  13.1 7.0 %all-to-all-start = ((bf16[4,6,2,16,1,512]{5,2,1,0,4,3:T(2,128)(2,1)}), bf16[4,6,2,16,1,512]{5,2,1,0,4,3:T(2,128)(2,1)S(1)}, u32[]{:S(2)}, u32[]{:S(2)}) async-start(bf16[4,6,2,16,1,512]{5,2,1,0,4,3:T(2,128)(2,1)} %broadcast_select_fusion), calls=%async_computation | async-start | bytes 1572864 | tf_op jit(solution)/shard_map/all_to_all | solution.py:180
  20.1 0.0 copy-done
  20.2 0.1 copy.14
  20.2 0.1 reshape_squeeze.3.shift_ref
  20.3 0.7 dynamic-slice_bitcast_fusion
  21.1 0.1 fusion
  21.1 0.1 reshape.67.live_ref
  21.2 13.4 %all-to-all-done = bf16[4,6,2,16,1,512]{5,2,1,0,4,3:T(2,128)(2,1)S(1)} async-done(((bf16[4,6,2,16,1,512]{5,2,1,0,4,3:T(2,128)(2,1)}), bf16[4,6,2,16,1,512]{5,2,1,0,4,3:T(2,128)(2,1)S(1)}, u32[]{:S(2)}, u32[]{:S(2)}) %all-to-all-start) | async-done | bytes 786464 | tf_op jit(solution)/shard_map/all_to_all | solution.py:180
  34.6 0.4 copy.22
  35.1 48.3 %all-gather.2.cloned.1.call-done.g_hbm = bf16[4,96,2,16,512]{4,3,2,1,0:T(8,128)(2,1)} async-done(((bf16[4,6,2,16,512]{4,3,2,1,0:T(8,128)(2,1)}), bf16[4,96,2,16,512]{4,3,2,1,0:T(8,128)(2,1)}) %all-gather.2.cloned.1.call-update) | async-done | bytes 12582928 | tf_op jit(solution)/shard_map/all_gather | solution.py:182
  83.4 79.7 %shard_map.55 = f32[4,6,2,16,512]{4,3,2,1,0:T(8,128)S(1)} custom-call(s32[48]{0:T(128)S(1)} %reshape_squeeze.3.shift_ref, f32[48]{0:T(128)S(1)} %reshape.67.live_ref, bf16[4,6,2,16,512]{4,3,2,1,0:T(8,128)(2,1)S(1)} %bitcast.15, bf16[4,96,2,16,512]{4,3,2,1,0:T(8,128)(2,1)} %all-gather.2.cloned.1.call-done.g_hbm), custom_call_target="tpu_custom_call" | custom-call | tf_op jit(solution)/shard_map/pallas_call | solution.py:146
  163.1 1.1 copy.25
  (4 shorter events, 0.0 us)
Async XLA Ops:
  6.5 13.6 %copy-start = (s32[16,16,3]{1,0,2:T(8,128)S(1)}, s32[16,16,3]{1,0,2:T(8,128)}, u32[]{:S(2)}) copy-start(s32[16,16,3]{1,0,2:T(8,128)} %param.8) | copy-start | bytes 9220
  6.5 76.8 %all-gather.2.cloned.1.call-start = ((), (), s32[]{:S(2)}) async-start(), calls=%async_computation.1 | async-start | bytes 13369344 | tf_op jit(solution)/shard_map/all_gather | solution.py:182
  13.1 21.5 %all-to-all-start = ((bf16[4,6,2,16,1,512]{5,2,1,0,4,3:T(2,128)(2,1)}), bf16[4,6,2,16,1,512]{5,2,1,0,4,3:T(2,128)(2,1)S(1)}, u32[]{:S(2)}, u32[]{:S(2)}) async-start(bf16[4,6,2,16,1,512]{5,2,1,0,4,3:T(2,128)(2,1)} %broadcast_select_fusion), calls=%async_computation | async-start | bytes 1572864 | tf_op jit(solution)/shard_map/all_to_all | solution.py:180
Sparse Core Ops, SparseCore 0:
  9.2 74.1 all-gather.1

commit v11 on v9

--- a/solution.py
+++ b/solution.py
@@ -163,6 +163,93 @@
     )(shifts, lives, owned, whole)
 
 
+def gather_kernel(chips, x_hbm, out_ref, local_sem, ring_send, ring_recv, pass_send, pass_recv):
+    halves = 2
+    per_energy = x_hbm.shape[1]
+    me = lax.axis_index("energy")
+    cell = lax.axis_index("cell")
+    chip, core = me // 2, me % 2
+    step_dir = 1 - 2 * core
+    partner = me + step_dir
+    ahead = 2 * ((chip + step_dir + chips) % chips) + core
+
+    def origin(k):
+        return 2 * ((chip - step_dir * k + chips) % chips) + core
+
+    def handed_group(k):
+        return 2 * ((chip + step_dir * k + chips) % chips) + 1 - core
+
+    def place(group, h):
+        return out_ref.at[pl.ds(2 * h, 2), pl.ds(group * per_energy, per_energy)]
+
+    def own_half(h):
+        return x_hbm.at[pl.ds(2 * h, 2)]
+
+    def remote(src, dst, send, recv, k, h, target):
+        return pltpu.make_async_remote_copy(
+            src_ref=src, dst_ref=dst, send_sem=send.at[k, h], recv_sem=recv.at[k, h],
+            device_id=(target, cell), device_id_type=pl.DeviceIdType.MESH,
+        )
+
+    def ring_copy(k, h):
+        src = own_half(h) if k == 1 else place(origin(k - 1), h)
+        return remote(src, place(origin(k - 1), h), ring_send, ring_recv, k, h, ahead)
+
+    def pass_copy(k, h):
+        src = own_half(h) if k == 0 else place(origin(k), h)
+        return remote(src, place(origin(k), h), pass_send, pass_recv, k, h, partner)
+
+    def arrival(k, h):
+        return remote(place(origin(k), h), place(origin(k), h), ring_send, ring_recv, k, h, ahead)
+
+    def handed(k, h):
+        slot = place(handed_group(k), h)
+        return remote(slot, slot, pass_send, pass_recv, k, h, partner)
+
+    locals_ = [pltpu.make_async_copy(own_half(h), place(me, h), local_sem.at[h]) for h in range(halves)]
+    for copy in locals_:
+        copy.start()
+    sends = [ring_copy(1, h) for h in range(halves)] + [pass_copy(0, h) for h in range(halves)]
+    for copy in sends:
+        copy.start()
+    for k in range(1, chips):
+        for h in range(halves):
+            arrival(k, h).wait_recv()
+            onward = [pass_copy(k, h)]
+            if k + 1 < chips:
+                onward.append(ring_copy(k + 1, h))
+            for copy in onward:
+                copy.start()
+            sends.extend(onward)
+    for k in range(chips):
+        for h in range(halves):
+            handed(k, h).wait_recv()
+    for copy in sends:
+        copy.wait_send()
+    for copy in locals_:
+        copy.wait()
+
+
+def ring_gather(block):
+    groups = lax.axis_size("energy")
+    chips = groups // 2
+    shape = (block.shape[0], groups * block.shape[1]) + block.shape[2:]
+    return pl.pallas_call(
+        functools.partial(gather_kernel, chips),
+        out_shape=jax.ShapeDtypeStruct(shape, block.dtype),
+        in_specs=[pl.BlockSpec(memory_space=pl.ANY)],
+        out_specs=pl.BlockSpec(memory_space=pl.ANY),
+        scratch_shapes=[
+            pltpu.SemaphoreType.DMA((2,)),
+            pltpu.SemaphoreType.DMA((chips, 2)),
+            pltpu.SemaphoreType.DMA((chips, 2)),
+            pltpu.SemaphoreType.DMA((chips, 2)),
+            pltpu.SemaphoreType.DMA((chips, 2)),
+        ],
+        compiler_params=pltpu.CompilerParams(has_side_effects=True),
+    )(block)
+
+
 def per_device(green, screened, cell_map, shift_table, shift_count):
     cell_count = lax.axis_size("cell")
     per_energy = green.shape[1]
@@ -173,7 +260,7 @@
     outgoing = outgoing.reshape(4, per_energy, per_cell, cell_count, screened.shape[3], width)
     arrived = lax.all_to_all(outgoing, "cell", split_axis=3, concat_axis=3, tiled=True)
     owned = arrived.reshape(4, per_energy, per_cell, green.shape[3], width)
-    whole = lax.all_gather(green, "energy", axis=1, tiled=True)
+    whole = ring_gather(green)
     group = lax.axis_index("energy")
     shifts, lives = slot_tables(shift_table, shift_count, group)
     return ring_convolve(shifts, lives, owned, whole, shift_table.shape[2])

time: 174 us -> 174 us (level)
  Pallas kernels: 79.8 us -> 156 us
  waiting for transfers between devices: 62.4 us -> 0.01 us
  between operations: 13.5 us -> 0.09 us
    pallas_call x0 -> x1, Pallas kernels: none -> 76 us  [ring_gather(): pl.pallas_call(functools.partial(gather_kernel, chips), out_shape=jax.Sha...]
    all_gather x1 -> x0, waiting for transfers between devices: 48.3 us -> none  [per_device(): whole = lax.all_gather(green, 'energy', axis=1, tiled=True)]
    all_to_all x1, waiting for transfers between devices: 13.4 us -> 0.01 us  [per_device(): lax.all_to_all(outgoing, 'cell', split_axis=3, concat_axis=3, tiled=True)]
  transfers between devices with their start and end apart: 2 -> 1, of which waited for: 2 -> 0; matrix products, arithmetic and copies ran while one was open for 4% -> 1% of each run, Pallas kernels for 0% -> 44%
where the time goes in v11:
time: 174 us; the launch traced here: 171 us
  Pallas kernels  156 us (90%)
  starting transfers between devices  7.03 us (4%)
  local copies, waits for them, and re-layouts  6.47 us (4%)
  other arithmetic  1.96 us (1%)
    pallas_call x1, Pallas kernels, ring_convolve(): pl.pallas_call(functools.partial(ring_conv_kernel, chips, slot_count), ou...  79.7 us
    pallas_call x1, Pallas kernels, ring_gather(): pl.pallas_call(functools.partial(gather_kernel, chips), out_shape=jax.Sha...  76 us
    all_to_all x1, starting transfers between devices, per_device(): lax.all_to_all(outgoing, 'cell', split_axis=3, concat_axis=3, tiled=True)  7.03 us
  transfers between devices with their start and end apart: 1, of which 0 were waited for; matrix products, arithmetic and copies ran while one was open for 1% of the time, Pallas kernels for 44%

profile of v11, /device:TPU:224, one launch (start us, length us, event | category | flops | bytes accessed | tf_op | source)
XLA Modules:
  0.0 171.3 jit_solution(9263602618663950033)
XLA Ops:
  0.0 0.0 copy-start
  0.0 0.7 reshape.64
  0.8 0.1 copy.16
  0.8 0.1 reshape.65
  0.9 1.7 %copy.23 = bf16[4,6,32,1,512]{4,0,2,1,3:T(4,128)(2,1)S(1)} copy(bf16[4,6,32,1,512]{4,2,3,1,0:T(8,128)(2,1)} %param.6) | data formatting | bytes 1572864 | tf_op args[1]
  2.7 1.3 gather_fusion
  4.0 1.9 %broadcast_select_fusion = bf16[4,6,2,16,1,512]{5,2,1,0,4,3:T(2,128)(2,1)} fusion(pred[2,16]{0,1:T(8,128)(4,1)S(1)} %compare_and_fusion, bf16[4,6,2,16,1,512]{5,0,1,3,2,4:T(4,128)(2,1)S(1)} %bitcast.16), kind=kLoop, calls=%fused_computation.1 | loop fusion | flops 393216 | bytes 1572896 | tf_op jit(solution)/shard_map/jit(_take)/select_n | solution.py:259
  5.8 7.0 %all-to-all-start = ((bf16[4,6,2,16,1,512]{5,2,1,0,4,3:T(2,128)(2,1)}), bf16[4,6,2,16,1,512]{5,2,1,0,4,3:T(2,128)(2,1)S(1)}, u32[]{:S(2)}, u32[]{:S(2)}) async-start(bf16[4,6,2,16,1,512]{5,2,1,0,4,3:T(2,128)(2,1)} %broadcast_select_fusion), calls=%async_computation | async-start | bytes 1572864 | tf_op jit(solution)/shard_map/all_to_all | solution.py:261
  12.9 0.0 copy-done
  12.9 0.1 copy.14
  13.0 0.1 reshape_squeeze.3.shift_ref
  13.1 0.7 dynamic-slice_bitcast_fusion
  13.8 0.1 fusion
  13.8 0.1 reshape.67.live_ref
  13.9 76.0 %shard_map.55.g_hbm = bf16[4,96,2,16,512]{4,3,2,1,0:T(8,128)(2,1)} custom-call(bf16[4,6,2,16,512]{4,3,2,1,0:T(8,128)(2,1)} %x_hbm.1), custom_call_target="tpu_custom_call" | custom-call | tf_op jit(solution)/shard_map/pallas_call | solution.py:237
  90.0 0.0 all-to-all-done
  90.0 0.4 copy.22
  90.4 79.7 %shard_map.56 = f32[4,6,2,16,512]{4,3,2,1,0:T(8,128)S(1)} custom-call(s32[48]{0:T(128)S(1)} %reshape_squeeze.3.shift_ref, f32[48]{0:T(128)S(1)} %reshape.67.live_ref, bf16[4,6,2,16,512]{4,3,2,1,0:T(8,128)(2,1)S(1)} %bitcast.15, bf16[4,96,2,16,512]{4,3,2,1,0:T(8,128)(2,1)} %shard_map.55.g_hbm), custom_call_target="tpu_custom_call" | custom-call | tf_op jit(solution)/shard_map/pallas_call | solution.py:140
  170.2 1.1 copy.25
  (4 shorter events, 0.0 us)
Async XLA Ops:
  0.0 12.9 %copy-start = (s32[16,16,3]{1,0,2:T(8,128)S(1)}, s32[16,16,3]{1,0,2:T(8,128)}, u32[]{:S(2)}) copy-start(s32[16,16,3]{1,0,2:T(8,128)} %param.8) | copy-start | bytes 9220
  5.8 84.2 %all-to-all-start = ((bf16[4,6,2,16,1,512]{5,2,1,0,4,3:T(2,128)(2,1)}), bf16[4,6,2,16,1,512]{5,2,1,0,4,3:T(2,128)(2,1)S(1)}, u32[]{:S(2)}, u32[]{:S(2)}) async-start(bf16[4,6,2,16,1,512]{5,2,1,0,4,3:T(2,128)(2,1)} %broadcast_select_fusion), calls=%async_computation | async-start | bytes 1572864 | tf_op jit(solution)/shard_map/all_to_all | solution.py:261

commit v12 on v11

--- a/solution.py
+++ b/solution.py
@@ -163,7 +163,8 @@
     )(shifts, lives, owned, whole)
 
 
-def gather_kernel(chips, x_hbm, out_ref, local_sem, ring_send, ring_recv, pass_send, pass_recv):
+def gather_kernel(chips, x_hbm, rows_hbm, out_ref, owned_ref, local_sem, ring_send, ring_recv,
+                  pass_send, pass_recv, row_send, row_recv, row_local):
     halves = 2
     per_energy = x_hbm.shape[1]
     me = lax.axis_index("energy")
@@ -205,6 +206,34 @@
     def handed(k, h):
         slot = place(handed_group(k), h)
         return remote(slot, slot, pass_send, pass_recv, k, h, partner)
+
+    peers = rows_hbm.shape[3]
+
+    def row_copy(d):
+        return pltpu.make_async_remote_copy(
+            src_ref=rows_hbm.at[:, :, :, pl.ds(d, 1)],
+            dst_ref=owned_ref.at[:, :, :, pl.ds(cell, 1)],
+            send_sem=row_send.at[d], recv_sem=row_recv.at[cell],
+            device_id=(me, d), device_id_type=pl.DeviceIdType.MESH,
+        )
+
+    def row_arrival(r):
+        return pltpu.make_async_remote_copy(
+            src_ref=owned_ref.at[:, :, :, pl.ds(r, 1)],
+            dst_ref=owned_ref.at[:, :, :, pl.ds(r, 1)],
+            send_sem=row_send.at[r], recv_sem=row_recv.at[r],
+            device_id=(me, r), device_id_type=pl.DeviceIdType.MESH,
+        )
+
+    own_rows = pltpu.make_async_copy(
+        rows_hbm.at[:, :, :, pl.ds(cell, 1)], owned_ref.at[:, :, :, pl.ds(cell, 1)], row_local
+    )
+    own_rows.start()
+    row_sends = []
+    for step in range(1, peers):
+        copy = row_copy((cell + step) % peers)
+        copy.start()
+        row_sends.append(copy)
 
     locals_ = [pltpu.make_async_copy(own_half(h), place(me, h), local_sem.at[h]) for h in range(halves)]
     for copy in locals_:
@@ -224,30 +253,42 @@
     for k in range(chips):
         for h in range(halves):
             handed(k, h).wait_recv()
+    for step in range(1, peers):
+        row_arrival((cell + peers - step) % peers).wait_recv()
+    for copy in row_sends:
+        copy.wait_send()
+    own_rows.wait()
     for copy in sends:
         copy.wait_send()
     for copy in locals_:
         copy.wait()
 
 
-def ring_gather(block):
+def ring_gather(block, rows):
     groups = lax.axis_size("energy")
+    peers = lax.axis_size("cell")
     chips = groups // 2
     shape = (block.shape[0], groups * block.shape[1]) + block.shape[2:]
     return pl.pallas_call(
         functools.partial(gather_kernel, chips),
-        out_shape=jax.ShapeDtypeStruct(shape, block.dtype),
-        in_specs=[pl.BlockSpec(memory_space=pl.ANY)],
-        out_specs=pl.BlockSpec(memory_space=pl.ANY),
+        out_shape=(
+            jax.ShapeDtypeStruct(shape, block.dtype),
+            jax.ShapeDtypeStruct(rows.shape, rows.dtype),
+        ),
+        in_specs=[pl.BlockSpec(memory_space=pl.ANY)] * 2,
+        out_specs=(pl.BlockSpec(memory_space=pl.ANY),) * 2,
         scratch_shapes=[
             pltpu.SemaphoreType.DMA((2,)),
             pltpu.SemaphoreType.DMA((chips, 2)),
             pltpu.SemaphoreType.DMA((chips, 2)),
             pltpu.SemaphoreType.DMA((chips, 2)),
             pltpu.SemaphoreType.DMA((chips, 2)),
+            pltpu.SemaphoreType.DMA((peers,)),
+            pltpu.SemaphoreType.DMA((peers,)),
+            pltpu.SemaphoreType.DMA(()),
         ],
         compiler_params=pltpu.CompilerParams(has_side_effects=True),
-    )(block)
+    )(block, rows)
 
 
 def per_device(green, screened, cell_map, shift_table, shift_count):
@@ -258,9 +299,8 @@
     wanted = jnp.transpose(cell_map.reshape(cell_count, per_cell)).reshape(-1)
     outgoing = jnp.take(screened, wanted, axis=2)
     outgoing = outgoing.reshape(4, per_energy, per_cell, cell_count, screened.shape[3], width)
-    arrived = lax.all_to_all(outgoing, "cell", split_axis=3, concat_axis=3, tiled=True)
+    whole, arrived = ring_gather(green, outgoing)
     owned = arrived.reshape(4, per_energy, per_cell, green.shape[3], width)
-    whole = ring_gather(green)
     group = lax.axis_index("energy")
     shifts, lives = slot_tables(shift_table, shift_count, group)
     return ring_convolve(shifts, lives, owned, whole, shift_table.shape[2])

time: 174 us -> 170 us (0.977)
  starting transfers between devices: 7.03 us -> 0 us
    all_to_all x1 -> x0, starting transfers between devices: 7.03 us -> none  [per_device(): lax.all_to_all(outgoing, 'cell', split_axis=3, concat_axis=3, tiled=True)]
    unnamed x4 -> x5, local copies, waits for them, and re-layouts: 2.9 us -> 4.62 us
  transfers between devices with their start and end apart: 1 -> 0, of which waited for: 0 -> 0; matrix products, arithmetic and copies ran while one was open for 1% -> 0% of each run, Pallas kernels for 44% -> 0%
where the time goes in v12:
time: 170 us; the launch traced here: 167 us
  Pallas kernels  156 us (92%)
  local copies, waits for them, and re-layouts  7.85 us (5%)
  other arithmetic  3.07 us (2%)
    pallas_call x1, Pallas kernels, ring_convolve(): pl.pallas_call(functools.partial(ring_conv_kernel, chips, slot_count), ou...  79.8 us
    pallas_call x1, Pallas kernels, ring_gather(): pl.pallas_call(functools.partial(gather_kernel, chips), out_shape=(jax.Sh...  76 us
    unnamed x5, local copies, waits for them, and re-layouts  4.62 us

profile of v12, /device:TPU:224, one launch (start us, length us, event | category | flops | bytes accessed | tf_op | source)
XLA Modules:
  0.0 166.8 jit_solution(3429365225291341384)
XLA Ops:
  0.0 0.0 copy-start
  0.0 0.7 dynamic-slice_bitcast_fusion
  0.7 0.1 copy-done
  0.8 0.1 copy.9
  0.8 0.1 reshape_squeeze.3.shift_ref
  0.9 0.1 fusion
  1.0 0.1 reshape.67.live_ref
  1.1 0.7 reshape.64
  1.8 0.1 copy.12
  1.9 0.1 reshape.65
  2.0 0.1 copy.10
  2.1 1.8 %copy.22 = bf16[4,6,32,1,512]{4,0,2,1,3:T(4,128)(2,1)S(1)} copy(bf16[4,6,32,1,512]{4,2,3,1,0:T(8,128)(2,1)} %param.6) | data formatting | bytes 1572864 | tf_op args[1]
  3.9 1.3 gather_fusion
  5.2 3.0 %broadcast_select_fusion.rows_hbm = bf16[4,6,2,16,1,512]{5,4,3,2,1,0:T(2,128)(2,1)} fusion(pred[2,16]{1,0:T(4,128)(4,1)S(1)} %copy.10, bf16[4,6,2,16,1,512]{5,0,1,3,2,4:T(4,128)(2,1)S(1)} %bitcast.16), kind=kLoop, calls=%fused_computation.1 | loop fusion | flops 393216 | bytes 1572896 | tf_op jit(solution)/shard_map/jit(_take)/select_n | solution.py:300
  8.1 76.0 %shard_map.55 = (bf16[4,96,2,16,512]{4,3,2,1,0:T(8,128)(2,1)}, bf16[4,6,2,16,1,512]{5,4,3,2,1,0:T(2,128)(2,1)}) custom-call(bf16[4,6,2,16,512]{4,3,2,1,0:T(8,128)(2,1)} %x_hbm.1, bf16[4,6,2,16,1,512]{5,4,3,2,1,0:T(2,128)(2,1)} %broadcast_select_fusion.rows_hbm), custom_call_target="tpu_custom_call" | custom-call | tf_op jit(solution)/shard_map/pallas_call | solution.py:272
  84.2 1.7 copy.21
  85.8 79.8 %shard_map.56 = f32[4,6,2,16,512]{4,3,2,1,0:T(8,128)S(1)} custom-call(s32[48]{0:T(128)S(1)} %reshape_squeeze.3.shift_ref, f32[48]{0:T(128)S(1)} %reshape.67.live_ref, bf16[4,6,2,16,512]{4,3,2,1,0:T(8,128)(2,1)S(1)} %bitcast.15, bf16[4,96,2,16,512]{4,3,2,1,0:T(8,128)(2,1)} %get-tuple-element.8.g_hbm), custom_call_target="tpu_custom_call" | custom-call | tf_op jit(solution)/shard_map/pallas_call | solution.py:140
  165.6 1.1 copy.24
  (4 shorter events, 0.0 us)
Async XLA Ops:
  0.0 0.8 copy-start

commit v13 on v12

--- a/solution.py
+++ b/solution.py
@@ -297,7 +297,7 @@
     per_cell = green.shape[2]
     width = green.shape[4]
     wanted = jnp.transpose(cell_map.reshape(cell_count, per_cell)).reshape(-1)
-    outgoing = jnp.take(screened, wanted, axis=2)
+    outgoing = jnp.take(screened, wanted, axis=2, mode="clip")
     outgoing = outgoing.reshape(4, per_energy, per_cell, cell_count, screened.shape[3], width)
     whole, arrived = ring_gather(green, outgoing)
     owned = arrived.reshape(4, per_energy, per_cell, green.shape[3], width)

time: 170 us -> 169 us (level)
  other arithmetic: 3.07 us -> 0.08 us
  local copies, waits for them, and re-layouts: 7.85 us -> 10.6 us
    select_n x2 -> x0, other arithmetic: 2.98 us -> none  [per_device(): outgoing = jnp.take(screened, wanted, axis=2)]
    reshape x0 -> x1, local copies, waits for them, and re-layouts: none -> 2.84 us  [per_device(): outgoing.reshape(4, per_energy, per_cell, cell_count, screened.shape[3],...]
where the time goes in v13:
time: 169 us; the launch traced here: 167 us
  Pallas kernels  156 us (92%)
  local copies, waits for them, and re-layouts  10.6 us (6%)
    pallas_call x1, Pallas kernels, ring_convolve(): pl.pallas_call(functools.partial(ring_conv_kernel, chips, slot_count), ou...  79.8 us
    pallas_call x1, Pallas kernels, ring_gather(): pl.pallas_call(functools.partial(gather_kernel, chips), out_shape=(jax.Sh...  76 us
    unnamed x5, local copies, waits for them, and re-layouts  4.62 us

profile of v13, /device:TPU:224, one launch (start us, length us, event | category | flops | bytes accessed | tf_op | source)
XLA Modules:
  0.0 166.5 jit_solution(7654620203115591284)
XLA Ops:
  0.0 0.0 copy-start
  0.0 0.7 dynamic-slice_bitcast_fusion
  0.7 0.1 copy-done
  0.8 0.1 copy.8
  0.8 0.1 reshape_squeeze.3.shift_ref
  0.9 0.1 fusion
  1.0 0.1 reshape.21.live_ref
  1.1 0.7 reshape.18
  1.8 0.1 copy.10
  1.9 0.1 reshape.26
  2.0 1.8 %copy.19 = bf16[4,6,32,1,512]{4,0,2,1,3:T(4,128)(2,1)S(1)} copy(bf16[4,6,32,1,512]{4,2,3,1,0:T(8,128)(2,1)} %param.6) | data formatting | bytes 1572864 | tf_op args[1]
  3.8 1.3 gather_fusion
  5.0 2.8 %copy.12.rows_hbm = bf16[4,6,2,16,1,512]{5,4,3,2,1,0:T(2,128)(2,1)} copy(bf16[4,6,2,16,1,512]{5,0,1,3,2,4:T(4,128)(2,1)S(1)} %bitcast.14) | data formatting | bytes 1572864 | tf_op jit(solution)/shard_map/reshape | solution.py:301
  7.9 76.0 %shard_map.55 = (bf16[4,96,2,16,512]{4,3,2,1,0:T(8,128)(2,1)}, bf16[4,6,2,16,1,512]{5,4,3,2,1,0:T(2,128)(2,1)}) custom-call(bf16[4,6,2,16,512]{4,3,2,1,0:T(8,128)(2,1)} %x_hbm.1, bf16[4,6,2,16,1,512]{5,4,3,2,1,0:T(2,128)(2,1)} %copy.12.rows_hbm), custom_call_target="tpu_custom_call" | custom-call | tf_op jit(solution)/shard_map/pallas_call | solution.py:272
  83.9 1.7 %copy.18 = bf16[4,6,2,16,1,512]{5,3,4,2,1,0:T(8,128)(2,1)S(1)} copy(bf16[4,6,2,16,1,512]{5,4,3,2,1,0:T(2,128)(2,1)} %get-tuple-element.7) | data formatting | bytes 1572864
  85.6 79.8 %shard_map.56 = f32[4,6,2,16,512]{4,3,2,1,0:T(8,128)S(1)} custom-call(s32[48]{0:T(128)S(1)} %reshape_squeeze.3.shift_ref, f32[48]{0:T(128)S(1)} %reshape.21.live_ref, bf16[4,6,2,16,512]{4,3,2,1,0:T(8,128)(2,1)S(1)} %bitcast.12, bf16[4,96,2,16,512]{4,3,2,1,0:T(8,128)(2,1)} %get-tuple-element.8.g_hbm), custom_call_target="tpu_custom_call" | custom-call | tf_op jit(solution)/shard_map/pallas_call | solution.py:140
  165.4 1.1 copy.21
  (2 shorter events, 0.0 us)
Async XLA Ops:
  0.0 0.8 copy-start

commit v14 on v13

--- a/solution.py
+++ b/solution.py
@@ -207,26 +207,26 @@
         slot = place(handed_group(k), h)
         return remote(slot, slot, pass_send, pass_recv, k, h, partner)
 
-    peers = rows_hbm.shape[3]
+    peers = rows_hbm.shape[0]
 
     def row_copy(d):
         return pltpu.make_async_remote_copy(
-            src_ref=rows_hbm.at[:, :, :, pl.ds(d, 1)],
-            dst_ref=owned_ref.at[:, :, :, pl.ds(cell, 1)],
+            src_ref=rows_hbm.at[d],
+            dst_ref=owned_ref.at[cell],
             send_sem=row_send.at[d], recv_sem=row_recv.at[cell],
             device_id=(me, d), device_id_type=pl.DeviceIdType.MESH,
         )
 
     def row_arrival(r):
         return pltpu.make_async_remote_copy(
-            src_ref=owned_ref.at[:, :, :, pl.ds(r, 1)],
-            dst_ref=owned_ref.at[:, :, :, pl.ds(r, 1)],
+            src_ref=owned_ref.at[r],
+            dst_ref=owned_ref.at[r],
             send_sem=row_send.at[r], recv_sem=row_recv.at[r],
             device_id=(me, r), device_id_type=pl.DeviceIdType.MESH,
         )
 
     own_rows = pltpu.make_async_copy(
-        rows_hbm.at[:, :, :, pl.ds(cell, 1)], owned_ref.at[:, :, :, pl.ds(cell, 1)], row_local
+        rows_hbm.at[cell], owned_ref.at[cell], row_local
     )
     own_rows.start()
     row_sends = []
@@ -296,11 +296,13 @@
     per_energy = green.shape[1]
     per_cell = green.shape[2]
     width = green.shape[4]
-    wanted = jnp.transpose(cell_map.reshape(cell_count, per_cell)).reshape(-1)
-    outgoing = jnp.take(screened, wanted, axis=2, mode="clip")
-    outgoing = outgoing.reshape(4, per_energy, per_cell, cell_count, screened.shape[3], width)
+    flat = screened.reshape(4, per_energy, screened.shape[2], width)
+    picked = jnp.take(flat, cell_map, axis=2)
+    picked = picked.reshape(4, per_energy, cell_count, per_cell, width)
+    outgoing = jnp.transpose(picked, (2, 0, 1, 3, 4)).reshape(cell_count, -1, width)
     whole, arrived = ring_gather(green, outgoing)
-    owned = arrived.reshape(4, per_energy, per_cell, green.shape[3], width)
+    arrived = arrived.reshape(cell_count, 4, per_energy, per_cell, width)
+    owned = jnp.transpose(arrived, (1, 2, 3, 0, 4))
     group = lax.axis_index("energy")
     shifts, lives = slot_tables(shift_table, shift_count, group)
     return ring_convolve(shifts, lives, owned, whole, shift_table.shape[2])

time: 169 us -> 169 us (level)
  local copies, waits for them, and re-layouts: 10.6 us -> 7.96 us
  other arithmetic: 0.08 us -> 2.25 us
    reshape x2 -> x1, local copies, waits for them, and re-layouts: 3.57 us -> 1.18 us  [per_device(): jnp.transpose(picked, (2, 0, 1, 3, 4)).reshape(cell_count, -1, width)]
    unnamed x5 -> x4, local copies, waits for them, and re-layouts: 4.62 us -> 2.9 us
where the time goes in v14:
time: 169 us; the launch traced here: 166 us
  Pallas kernels  156 us (92%)
  local copies, waits for them, and re-layouts  7.96 us (5%)
  other arithmetic  2.25 us (1%)
    pallas_call x1, Pallas kernels, ring_convolve(): pl.pallas_call(functools.partial(ring_conv_kernel, chips, slot_count), ou...  79.8 us
    pallas_call x1, Pallas kernels, ring_gather(): pl.pallas_call(functools.partial(gather_kernel, chips), out_shape=(jax.Sh...  76 us

profile of v14, /device:TPU:224, one launch (start us, length us, event | category | flops | bytes accessed | tf_op | source)
XLA Modules:
  0.0 166.1 jit_solution(12650476740771703770)
XLA Ops:
  0.0 0.0 copy-start
  0.0 0.7 dynamic-slice_bitcast_fusion
  0.7 0.7 compare_and_fusion
  1.4 0.7 compare_select_fusion
  2.0 0.0 copy-done
  2.0 0.1 broadcast_in_dim.14
  2.1 0.1 copy.9
  2.2 0.1 reshape_squeeze.3.shift_ref
  2.3 0.1 fusion.1
  2.4 0.1 reshape.28.live_ref
  2.5 1.7 %copy.15 = bf16[4,6,32,1,512]{4,0,2,1,3:T(4,128)(2,1)S(1)} copy(bf16[4,6,32,1,512]{4,2,3,1,0:T(8,128)(2,1)} %param.6) | data formatting | bytes 1572864 | tf_op args[1]
  4.2 1.3 gather_fusion
  5.5 0.9 fusion
  6.4 1.2 reshape.26.rows_hbm
  7.5 76.0 %shard_map.55 = (bf16[4,96,2,16,512]{4,3,2,1,0:T(8,128)(2,1)}, bf16[16,48,512]{2,1,0:T(8,128)(2,1)}) custom-call(bf16[4,6,2,16,512]{4,3,2,1,0:T(8,128)(2,1)} %x_hbm.1, bf16[16,48,512]{2,1,0:T(8,128)(2,1)} %reshape.26.rows_hbm), custom_call_target="tpu_custom_call" | custom-call | tf_op jit(solution)/shard_map/pallas_call | solution.py:272
  83.6 1.6 copy.12
  85.1 79.8 %shard_map.56 = f32[4,6,2,16,512]{4,3,2,1,0:T(8,128)S(1)} custom-call(s32[48]{0:T(128)S(1)} %reshape_squeeze.3.shift_ref, f32[48]{0:T(128)S(1)} %reshape.28.live_ref, bf16[4,6,2,16,512]{4,3,2,1,0:T(8,128)(2,1)S(1)} %bitcast.13, bf16[4,96,2,16,512]{4,3,2,1,0:T(8,128)(2,1)} %get-tuple-element.8.g_hbm), custom_call_target="tpu_custom_call" | custom-call | tf_op jit(solution)/shard_map/pallas_call | solution.py:140
  164.9 1.1 copy.17
  (2 shorter events, 0.0 us)
Async XLA Ops:
  0.0 2.0 %copy-start = (s32[16,16,3]{1,0,2:T(8,128)S(1)}, s32[16,16,3]{1,0,2:T(8,128)}, u32[]{:S(2)}) copy-start(s32[16,16,3]{1,0,2:T(8,128)} %param.8) | copy-start | bytes 9220

commit v15 on v14

--- a/solution.py
+++ b/solution.py
@@ -11,14 +11,7 @@
 LANES = 128
 
 
-def slot_tables(shift_table, shift_count, group):
-    groups, slot_count = shift_table.shape[1], shift_table.shape[2]
-    slot = lax.broadcasted_iota(jnp.int32, (groups, slot_count), 1)
-    live = (slot < shift_count[group][:, None]).astype(jnp.float32)
-    return shift_table[group].reshape(-1), live.reshape(-1)
-
-
-def ring_conv_kernel(chips, slot_count, shift_ref, live_ref, w_hbm, g_hbm, o_ref, g_vmem, *scratch):
+def ring_conv_kernel(chips, slot_count, shift_ref, count_ref, w_hbm, g_hbm, o_ref, g_vmem, *scratch):
     halves = 2
     count = 2 * chips
     bufs = [scratch[h * count:(h + 1) * count] for h in range(halves)]
@@ -34,6 +27,7 @@
     partner = me + step_dir
     ahead = 2 * ((chip + step_dir + chips) % chips) + core
     base = me * per_energy
+    groups = 2 * chips
 
     def origin(k):
         return 2 * ((chip - step_dir * k + chips) % chips) + core
@@ -76,8 +70,9 @@
                         real = jnp.zeros((rows, LANES), jnp.float32)
                         imag = jnp.zeros((rows, LANES), jnp.float32)
                         for c in range(slot_count):
-                            j = shift_ref[source * slot_count + c]
-                            weight = live_ref[source * slot_count + c]
+                            j = shift_ref[(me * groups + source) * slot_count + c]
+                            live = c < count_ref[me * groups + source]
+                            weight = jnp.where(live, 1.0, 0.0).astype(jnp.float32)
                             u = lag + e - j
                             if masked:
                                 weight = jnp.where(u >= 0, weight, 0.0)
@@ -133,7 +128,7 @@
     o_ref[...] = o_ref[...] * SCALE
 
 
-def ring_convolve(shifts, lives, owned, whole, slot_count):
+def ring_convolve(shifts, counts, owned, whole, slot_count):
     groups = lax.axis_size("energy")
     chips = groups // 2
     half = pltpu.VMEM((owned.shape[0] // 2,) + owned.shape[1:], owned.dtype)
@@ -160,7 +155,7 @@
         compiler_params=pltpu.CompilerParams(
             has_side_effects=True, vmem_limit_bytes=48 * 1024 * 1024
         ),
-    )(shifts, lives, owned, whole)
+    )(shifts, counts, owned, whole)
 
 
 def gather_kernel(chips, x_hbm, rows_hbm, out_ref, owned_ref, local_sem, ring_send, ring_recv,
@@ -297,15 +292,15 @@
     per_cell = green.shape[2]
     width = green.shape[4]
     flat = screened.reshape(4, per_energy, screened.shape[2], width)
-    picked = jnp.take(flat, cell_map, axis=2)
+    picked = jnp.take(flat, cell_map, axis=2, mode="clip")
     picked = picked.reshape(4, per_energy, cell_count, per_cell, width)
     outgoing = jnp.transpose(picked, (2, 0, 1, 3, 4)).reshape(cell_count, -1, width)
     whole, arrived = ring_gather(green, outgoing)
     arrived = arrived.reshape(cell_count, 4, per_energy, per_cell, width)
     owned = jnp.transpose(arrived, (1, 2, 3, 0, 4))
-    group = lax.axis_index("energy")
-    shifts, lives = slot_tables(shift_table, shift_count, group)
-    return ring_convolve(shifts, lives, owned, whole, shift_table.shape[2])
+    return ring_convolve(
+        shift_table.reshape(-1), shift_count.reshape(-1), owned, whole, shift_table.shape[2]
+    )
 
 
 def solution(mesh):

time: 169 us -> 169 us (level)
    reshape x0 -> x3, local copies, waits for them, and re-layouts: none -> 1.7 us  [the longest x1 0.77 us: per_device(): shift_count.reshape(-1)]
    unnamed x4 -> x3, local copies, waits for them, and re-layouts: 2.9 us -> 3.79 us
where the time goes in v15:
time: 169 us; the launch traced here: 166 us
  Pallas kernels  156 us (92%)
  local copies, waits for them, and re-layouts  9.51 us (6%)
    pallas_call x1, Pallas kernels, ring_convolve(): pl.pallas_call(functools.partial(ring_conv_kernel, chips, slot_count), ou...  80.2 us
    pallas_call x1, Pallas kernels, ring_gather(): pl.pallas_call(functools.partial(gather_kernel, chips), out_shape=(jax.Sh...  76 us
    unnamed x3, local copies, waits for them, and re-layouts  3.79 us

profile of v15, /device:TPU:224, one launch (start us, length us, event | category | flops | bytes accessed | tf_op | source)
XLA Modules:
  0.0 166.5 jit_solution(254114894582801424)
XLA Ops:
  0.0 0.8 reshape.19.count_ref
  0.8 0.7 pad_clamp_fusion
  1.4 0.9 copy.8
  2.3 0.2 reshape.18.shift_ref
  2.5 1.7 %copy.15 = bf16[4,6,32,1,512]{4,0,2,1,3:T(4,128)(2,1)S(1)} copy(bf16[4,6,32,1,512]{4,2,3,1,0:T(8,128)(2,1)} %param.6) | data formatting | bytes 1572864 | tf_op args[1]
  4.3 1.3 gather_fusion
  5.6 0.7 copy.14
  6.3 1.2 reshape.22.rows_hbm
  7.5 76.0 %shard_map.55 = (bf16[4,96,2,16,512]{4,3,2,1,0:T(8,128)(2,1)}, bf16[16,48,512]{2,1,0:T(8,128)(2,1)}) custom-call(bf16[4,6,2,16,512]{4,3,2,1,0:T(8,128)(2,1)} %x_hbm.1, bf16[16,48,512]{2,1,0:T(8,128)(2,1)} %reshape.22.rows_hbm), custom_call_target="tpu_custom_call" | custom-call | tf_op jit(solution)/shard_map/pallas_call | solution.py:267
  83.5 1.6 copy.11
  85.1 80.2 %shard_map.56 = f32[4,6,2,16,512]{4,3,2,1,0:T(8,128)S(1)} custom-call(s32[768]{0:T(1024)S(1)} %reshape.18.shift_ref, s32[256]{0:T(256)S(1)} %reshape.19.count_ref, bf16[4,6,2,16,512]{4,3,2,1,0:T(8,128)(2,1)S(1)} %bitcast.12, bf16[4,96,2,16,512]{4,3,2,1,0:T(8,128)(2,1)} %get-tuple-element.8.g_hbm), custom_call_target="tpu_custom_call" | custom-call | tf_op jit(solution)/shard_map/pallas_call | solution.py:135
  165.3 1.1 copy.17

commit v16 on v14

--- a/solution.py
+++ b/solution.py
@@ -18,14 +18,14 @@
     return shift_table[group].reshape(-1), live.reshape(-1)
 
 
-def ring_conv_kernel(chips, slot_count, shift_ref, live_ref, w_hbm, g_hbm, o_ref, g_vmem, *scratch):
+def ring_conv_kernel(chips, slot_count, shift_ref, live_ref, w_hbm, g_hbm, out_hbm, o_ref, g_vmem, *scratch):
     halves = 2
     count = 2 * chips
     bufs = [scratch[h * count:(h + 1) * count] for h in range(halves)]
     own_bufs = [b[0] for b in bufs]
     ring_bufs = [(None,) + tuple(b[1:chips]) for b in bufs]
     hand_bufs = [tuple(b[chips:count]) for b in bufs]
-    g_sem, local_sem, ring_send, ring_recv, pass_send, pass_recv = scratch[halves * count:]
+    g_sem, local_sem, ring_send, ring_recv, pass_send, pass_recv, out_sem = scratch[halves * count:]
     comps, per_energy, positions, rows, width = o_ref.shape
     me = lax.axis_index("energy")
     cell = lax.axis_index("cell")
@@ -125,12 +125,19 @@
         for h in range(halves):
             handed(k - 1, h).wait_recv()
             compute(handed_group(k - 1), hand_bufs[h][k - 1], h, False)
+    outs = []
     for h in range(halves):
         handed(chips - 1, h).wait_recv()
         compute(handed_group(chips - 1), hand_bufs[h][chips - 1], h, False)
+        kind = pl.ds(2 * h, 2)
+        o_ref[kind] = o_ref[kind] * SCALE
+        copy = pltpu.make_async_copy(o_ref.at[kind], out_hbm.at[kind], out_sem.at[h])
+        copy.start()
+        outs.append(copy)
     for copy in sends:
         copy.wait_send()
-    o_ref[...] = o_ref[...] * SCALE
+    for copy in outs:
+        copy.wait()
 
 
 def ring_convolve(shifts, lives, owned, whole, slot_count):
@@ -146,8 +153,8 @@
             pl.BlockSpec(memory_space=pl.ANY),
             pl.BlockSpec(memory_space=pl.ANY),
         ],
-        out_specs=pl.BlockSpec(memory_space=pltpu.VMEM),
-        scratch_shapes=[pltpu.VMEM(whole.shape, whole.dtype)]
+        out_specs=pl.BlockSpec(memory_space=pl.ANY),
+        scratch_shapes=[pltpu.VMEM(owned.shape, jnp.float32), pltpu.VMEM(whole.shape, whole.dtype)]
         + [half] * (4 * chips)
         + [
             pltpu.SemaphoreType.DMA(()),
@@ -156,6 +163,7 @@
             pltpu.SemaphoreType.DMA((chips, 2)),
             pltpu.SemaphoreType.DMA((chips, 2)),
             pltpu.SemaphoreType.DMA((chips, 2)),
+            pltpu.SemaphoreType.DMA((2,)),
         ],
         compiler_params=pltpu.CompilerParams(
             has_side_effects=True, vmem_limit_bytes=48 * 1024 * 1024

time: 169 us -> 169 us (level)
  no operation moved by 1% of the time
where the time goes in v16:
time: 169 us; the launch traced here: 166 us
  Pallas kernels  156 us (92%)
  local copies, waits for them, and re-layouts  7.96 us (5%)
  other arithmetic  2.25 us (1%)
    pallas_call x1, Pallas kernels, ring_convolve(): pl.pallas_call(functools.partial(ring_conv_kernel, chips, slot_count), ou...  80 us
    pallas_call x1, Pallas kernels, ring_gather(): pl.pallas_call(functools.partial(gather_kernel, chips), out_shape=(jax.Sh...  76 us

profile of v16, /device:TPU:224, one launch (start us, length us, event | category | flops | bytes accessed | tf_op | source)
XLA Modules:
  0.0 166.3 jit_solution(4123020062139547099)
XLA Ops:
  0.0 0.0 copy-start
  0.0 0.7 dynamic-slice_bitcast_fusion
  0.7 0.7 compare_and_fusion
  1.4 0.7 compare_select_fusion
  2.0 0.0 copy-done
  2.0 0.1 broadcast_in_dim.14
  2.1 0.1 copy.9
  2.2 0.1 reshape_squeeze.3.shift_ref
  2.3 0.1 fusion.1
  2.4 0.1 reshape.28.live_ref
  2.5 1.7 %copy.15 = bf16[4,6,32,1,512]{4,0,2,1,3:T(4,128)(2,1)S(1)} copy(bf16[4,6,32,1,512]{4,2,3,1,0:T(8,128)(2,1)} %param.6) | data formatting | bytes 1572864 | tf_op args[1]
  4.2 1.3 gather_fusion
  5.5 0.9 fusion
  6.4 1.2 reshape.26.rows_hbm
  7.5 76.0 %shard_map.55 = (bf16[4,96,2,16,512]{4,3,2,1,0:T(8,128)(2,1)}, bf16[16,48,512]{2,1,0:T(8,128)(2,1)}) custom-call(bf16[4,6,2,16,512]{4,3,2,1,0:T(8,128)(2,1)} %x_hbm.1, bf16[16,48,512]{2,1,0:T(8,128)(2,1)} %reshape.26.rows_hbm), custom_call_target="tpu_custom_call" | custom-call | tf_op jit(solution)/shard_map/pallas_call | solution.py:280
  83.6 1.6 copy.12
  85.1 80.0 %shard_map.56 = f32[4,6,2,16,512]{4,3,2,1,0:T(8,128)S(1)} custom-call(s32[48]{0:T(128)S(1)} %reshape_squeeze.3.shift_ref, f32[48]{0:T(128)S(1)} %reshape.28.live_ref, bf16[4,6,2,16,512]{4,3,2,1,0:T(8,128)(2,1)S(1)} %bitcast.13, bf16[4,96,2,16,512]{4,3,2,1,0:T(8,128)(2,1)} %get-tuple-element.8.g_hbm), custom_call_target="tpu_custom_call" | custom-call | tf_op jit(solution)/shard_map/pallas_call | solution.py:147
  165.1 1.1 copy.17
  (2 shorter events, 0.0 us)
Async XLA Ops:
  0.0 2.0 %copy-start = (s32[16,16,3]{1,0,2:T(8,128)S(1)}, s32[16,16,3]{1,0,2:T(8,128)}, u32[]{:S(2)}) copy-start(s32[16,16,3]{1,0,2:T(8,128)} %param.8) | copy-start | bytes 9220

commit v17 on v14

--- a/solution.py
+++ b/solution.py
@@ -297,7 +297,7 @@
     per_cell = green.shape[2]
     width = green.shape[4]
     flat = screened.reshape(4, per_energy, screened.shape[2], width)
-    picked = jnp.take(flat, cell_map, axis=2)
+    picked = jnp.take(flat, cell_map, axis=2, mode="clip")
     picked = picked.reshape(4, per_energy, cell_count, per_cell, width)
     outgoing = jnp.transpose(picked, (2, 0, 1, 3, 4)).reshape(cell_count, -1, width)
     whole, arrived = ring_gather(green, outgoing)

time: 169 us -> 168 us (level)
  no operation moved by 1% of the time
where the time goes in v17:
time: 168 us; the launch traced here: 165 us
  Pallas kernels  156 us (93%)
  local copies, waits for them, and re-layouts  8.65 us (5%)
    pallas_call x1, Pallas kernels, ring_convolve(): pl.pallas_call(functools.partial(ring_conv_kernel, chips, slot_count), ou...  79.8 us
    pallas_call x1, Pallas kernels, ring_gather(): pl.pallas_call(functools.partial(gather_kernel, chips), out_shape=(jax.Sh...  76 us

profile of v17, /device:TPU:224, one launch (start us, length us, event | category | flops | bytes accessed | tf_op | source)
XLA Modules:
  0.0 165.2 jit_solution(12620133245912204432)
XLA Ops:
  0.0 0.0 copy-start
  0.0 0.7 dynamic-slice_bitcast_fusion
  0.7 0.1 copy-done
  0.8 0.7 pad_clamp_fusion
  1.4 0.1 copy.9
  1.5 0.1 reshape_squeeze.3.shift_ref
  1.6 0.1 fusion
  1.7 0.1 reshape.23.live_ref
  1.8 1.7 %copy.16 = bf16[4,6,32,1,512]{4,0,2,1,3:T(4,128)(2,1)S(1)} copy(bf16[4,6,32,1,512]{4,2,3,1,0:T(8,128)(2,1)} %param.6) | data formatting | bytes 1572864 | tf_op args[1]
  3.5 1.3 gather_fusion
  4.8 0.7 copy.15
  5.5 1.2 reshape.21.rows_hbm
  6.7 76.0 %shard_map.55 = (bf16[4,96,2,16,512]{4,3,2,1,0:T(8,128)(2,1)}, bf16[16,48,512]{2,1,0:T(8,128)(2,1)}) custom-call(bf16[4,6,2,16,512]{4,3,2,1,0:T(8,128)(2,1)} %x_hbm.1, bf16[16,48,512]{2,1,0:T(8,128)(2,1)} %reshape.21.rows_hbm), custom_call_target="tpu_custom_call" | custom-call | tf_op jit(solution)/shard_map/pallas_call | solution.py:272
  82.7 1.6 copy.12
  84.3 79.8 %shard_map.56 = f32[4,6,2,16,512]{4,3,2,1,0:T(8,128)S(1)} custom-call(s32[48]{0:T(128)S(1)} %reshape_squeeze.3.shift_ref, f32[48]{0:T(128)S(1)} %reshape.23.live_ref, bf16[4,6,2,16,512]{4,3,2,1,0:T(8,128)(2,1)S(1)} %bitcast.14, bf16[4,96,2,16,512]{4,3,2,1,0:T(8,128)(2,1)} %get-tuple-element.8.g_hbm), custom_call_target="tpu_custom_call" | custom-call | tf_op jit(solution)/shard_map/pallas_call | solution.py:140
  164.1 1.1 copy.18
  (1 shorter events, 0.0 us)
Async XLA Ops:
  0.0 0.8 copy-start

commit v18 on v17

--- a/solution.py
+++ b/solution.py
@@ -299,7 +299,7 @@
     flat = screened.reshape(4, per_energy, screened.shape[2], width)
     picked = jnp.take(flat, cell_map, axis=2, mode="clip")
     picked = picked.reshape(4, per_energy, cell_count, per_cell, width)
-    outgoing = jnp.transpose(picked, (2, 0, 1, 3, 4)).reshape(cell_count, -1, width)
+    outgoing = jnp.transpose(picked, (2, 0, 1, 3, 4))
     whole, arrived = ring_gather(green, outgoing)
     arrived = arrived.reshape(cell_count, 4, per_energy, per_cell, width)
     owned = jnp.transpose(arrived, (1, 2, 3, 0, 4))

time: 168 us -> 168 us (level)
  no operation moved by 1% of the time
where the time goes in v18:
time: 168 us; the launch traced here: 165 us
  Pallas kernels  156 us (93%)
  local copies, waits for them, and re-layouts  8.33 us (5%)
    pallas_call x1, Pallas kernels, ring_convolve(): pl.pallas_call(functools.partial(ring_conv_kernel, chips, slot_count), ou...  79.8 us
    pallas_call x1, Pallas kernels, ring_gather(): pl.pallas_call(functools.partial(gather_kernel, chips), out_shape=(jax.Sh...  76 us

profile of v18, /device:TPU:224, one launch (start us, length us, event | category | flops | bytes accessed | tf_op | source)
XLA Modules:
  0.0 164.9 jit_solution(2890511039604914422)
XLA Ops:
  0.0 0.0 copy-start
  0.0 0.7 dynamic-slice_bitcast_fusion
  0.7 0.1 copy-done
  0.8 0.7 pad_clamp_fusion
  1.4 0.1 copy.8
  1.5 0.1 reshape_squeeze.3.shift_ref
  1.6 0.1 fusion
  1.7 0.1 reshape.15.live_ref
  1.8 1.7 %copy.20 = bf16[4,6,32,1,512]{4,0,2,1,3:T(4,128)(2,1)S(1)} copy(bf16[4,6,32,1,512]{4,2,3,1,0:T(8,128)(2,1)} %param.6) | data formatting | bytes 1572864 | tf_op args[1]
  3.5 1.3 gather_fusion
  4.8 1.6 copy.18
  6.4 76.0 %shard_map.55 = (bf16[4,96,2,16,512]{4,3,2,1,0:T(8,128)(2,1)}, bf16[16,4,6,2,512]{4,3,2,1,0:T(2,128)(2,1)}) custom-call(bf16[4,6,2,16,512]{4,3,2,1,0:T(8,128)(2,1)} %x_hbm.1, bf16[16,4,6,2,512]{4,3,2,1,0:T(2,128)(2,1)} %bitcast.15), custom_call_target="tpu_custom_call" | custom-call | tf_op jit(solution)/shard_map/pallas_call | solution.py:272
  82.4 1.6 copy.19
  84.0 79.8 %shard_map.56 = f32[4,6,2,16,512]{4,3,2,1,0:T(8,128)S(1)} custom-call(s32[48]{0:T(128)S(1)} %reshape_squeeze.3.shift_ref, f32[48]{0:T(128)S(1)} %reshape.15.live_ref, bf16[4,6,2,16,512]{4,3,2,1,0:T(8,128)(2,1)S(1)} %bitcast.14, bf16[4,96,2,16,512]{4,3,2,1,0:T(8,128)(2,1)} %get-tuple-element.8.g_hbm), custom_call_target="tpu_custom_call" | custom-call | tf_op jit(solution)/shard_map/pallas_call | solution.py:140
  163.8 1.1 copy.22
  (1 shorter events, 0.0 us)
Async XLA Ops:
  0.0 0.8 copy-start
